TPU v7x, 512 devices: a whole 4x4x16 slice. The times are simulated.
512 devices in a mesh: gx: 16 (over x, z_hi, core), gy: 32 (over z_lo, y).
Axes of the slice: x: 4, y: 4, z: 16 (z_hi: 2, z_lo: 8; z = z_hi * 8 + z_lo), core: 2. Of those that a mesh axis runs over, the one named last changes fastest.
Arguments:
- damage: float32 [256, 256, 512], P('gx', 'gy'), may hold values from 0 to 0.9
- strain: float32 [3, 256, 256, 512], P(None, 'gx', 'gy'), may hold values from -3 to 3
- seed_damage: float32 [256, 256, 512], P('gx', 'gy'), may hold values from -6 to 6
- seed_disp: float32 [3, 256, 256, 512], P(None, 'gx', 'gy'), may hold values from -6 to 6
- brick_work: int32 [16, 32], P('gx', 'gy'), may hold values from 1 to 4, as said below
Outputs:
- adjoint_damage: float32 [256, 256, 512], P('gx', 'gy')
- adjoint_disp: float32 [3, 256, 256, 512], P(None, 'gx', 'gy')
Inputs may be any that keep to these rules, and one draw needn't show every extreme that they name: brick_work is 1 on ordinary bricks and 2 to 4 on crack-band bricks. In every row of bricks (one gx index) the crack-band bricks form one run of 8 neighbouring bricks, all with gy index below 16. Some brick has weight 4.
All inputs are finite; a program needn't handle non-finite values.
Results may differ from a plain program's by a relative error of at most 0.0001.
Values sent between devices are 32-bit elements; how exact they have to be, the bound alone decides.
A program may use at most 64 MiB of HBM per device.

v0:
```python
import jax
import jax.numpy as jnp
from jax import lax
from jax.sharding import PartitionSpec as P

SWEEPS = 3
RELAX_INNER = 8


RESIDUAL_STIFFNESS = 0.001
TOUGH_OVER_LENGTH = 0.5
TOUGH_TIMES_LENGTH = 0.25
MASS_SHIFT = 0.5
STIFF_SCALE = 0.25
CENTER_VALUE = 1.0
HALF_WIDTH = 0.75
NORMAL_WEIGHT = 1.5
RELAX_STEP = 0.5
NORMAL_FLOOR = 0.05


def padded_2(block, sides, width):
    for axis, dim in sides:
        count = lax.axis_size(axis)
        forward = [(i, i + 1) for i in range(count - 1)]
        backward = [(target, source) for source, target in forward]
        low = lax.ppermute(
            lax.slice_in_dim(block, block.shape[dim] - width, None, axis=dim), axis, forward
        )
        high = lax.ppermute(lax.slice_in_dim(block, 0, width, axis=dim), axis, backward)
        block = jnp.concatenate([low, block, high], axis=dim)
    return block


def shifted(field):
    center = field[..., 1:-1, 1:-1, :]
    widths = [(0, 0)] * (center.ndim - 1) + [(1, 1)]
    padded = jnp.pad(center, widths)
    sides = [
        field[..., 2:, 1:-1, :],
        field[..., :-2, 1:-1, :],
        field[..., 1:-1, 2:, :],
        field[..., 1:-1, :-2, :],
        padded[..., 2:],
        padded[..., :-2],
    ]
    return (center, sides)


def prepare(framed_damage, framed_strain):
    center, sides = shifted(framed_damage)
    soft_center = (1.0 - center) ** 2 + RESIDUAL_STIFFNESS
    faces = jnp.stack(
        [0.5 * (soft_center + (1.0 - side) ** 2 + RESIDUAL_STIFFNESS) for side in sides]
    )
    energy = 0.5 * jnp.sum(framed_strain[:, 1:-1, 1:-1, :] ** 2, axis=0)
    coupling = 2.0 * (framed_damage - 1.0)[None] * framed_strain
    inverse_damage = 1.0 / (TOUGH_OVER_LENGTH + 2.0 * energy + 6.0 * TOUGH_TIMES_LENGTH)
    inverse_disp = 1.0 / (MASS_SHIFT + STIFF_SCALE * jnp.sum(faces, axis=0))
    inverse = jnp.stack([inverse_damage, inverse_disp, inverse_disp, inverse_disp])
    return (faces, energy, coupling, inverse)


def operate(faces, energy, coupling, state):
    mu_center, mu_sides = shifted(state[0])
    damage_part = (TOUGH_OVER_LENGTH + 2.0 * energy) * mu_center + TOUGH_TIMES_LENGTH * sum(
        (mu_center - side for side in mu_sides)
    )
    lam_center, lam_sides = shifted(state[1:])
    disp_part = MASS_SHIFT * lam_center + STIFF_SCALE * sum(
        (faces[slot] * (lam_center - lam_sides[slot]) for slot in range(6))
    )
    weighted = coupling * state[0][None]
    along_x = 0.5 * (weighted[0, :-2, 1:-1, :] - weighted[0, 2:, 1:-1, :])
    along_y = 0.5 * (weighted[1, 1:-1, :-2, :] - weighted[1, 1:-1, 2:, :])
    padded = jnp.pad(weighted[2, 1:-1, 1:-1, :], ((0, 0), (0, 0), (1, 1)))
    along_z = 0.5 * (padded[..., :-2] - padded[..., 2:])
    transfer = jnp.stack([along_x, along_y, along_z])
    return jnp.concatenate([damage_part[None], disp_part + transfer], axis=0)


def chebyshev(faces, energy, coupling, inverse, source, widen, keep):
    ratio = CENTER_VALUE / HALF_WIDTH
    rho = 1.0 / ratio
    update = inverse * source / CENTER_VALUE
    state = keep(update)
    for sweep in range(SWEEPS):
        residual = source - operate(faces, energy, coupling, widen(state))
        rho_next = 1.0 / (2.0 * ratio - rho)
        update = rho_next * rho * update + 2.0 * rho_next / HALF_WIDTH * inverse * residual
        state = keep(state + update)
        rho = rho_next
    return state


def crack_normal(framed_damage):
    center, sides = shifted(framed_damage)
    grad = jnp.stack(
        [0.5 * (sides[0] - sides[1]), 0.5 * (sides[2] - sides[3]), 0.5 * (sides[4] - sides[5])]
    )
    length = jnp.sqrt(jnp.maximum(jnp.sum(grad * grad, axis=0, keepdims=True), NORMAL_FLOOR))
    return grad / length


def relax_once(target, normal, relaxed):
    along = jnp.sum(normal * relaxed, axis=0, keepdims=True)
    return relaxed + RELAX_STEP / RELAX_INNER * (target - relaxed - NORMAL_WEIGHT * along * normal)


def relax(target, normal, count):

    def advance(level, relaxed):
        return relax_once(target, normal, relaxed)

    return lax.fori_loop(0, count * RELAX_INNER, advance, target)


def unchanged(state):
    return state


def body(damage, strain, seed_damage, seed_disp, brick_work):
    framed = padded_2(jnp.stack([damage, strain[0], strain[1]]), (("gx", 1), ("gy", 2)), 1)
    framed_damage = framed[0]
    framed_strain = jnp.stack([framed[1], framed[2], jnp.pad(strain[2], ((1, 1), (1, 1), (0, 0)))])
    faces, energy, coupling, inverse = prepare(framed_damage, framed_strain)
    source = jnp.concatenate([seed_damage[None], seed_disp], axis=0)

    def widen_faces(state):
        return padded_2(state, (("gx", 1), ("gy", 2)), 1)

    state = chebyshev(faces, energy, coupling, inverse, source, widen_faces, unchanged)
    normal = crack_normal(framed_damage)
    target = state[1:]
    own = brick_work[0, 0]
    corrected = relax(target, normal, own)
    return (state[0], corrected)


def solution(mesh):
    placed = (
        P("gx", "gy", None),
        P(None, "gx", "gy", None),
        P("gx", "gy", None),
        P(None, "gx", "gy", None),
        P("gx", "gy"),
    )
    return jax.shard_map(
        body,
        mesh=mesh,
        in_specs=placed,
        out_specs=(P("gx", "gy", None), P(None, "gx", "gy", None)),
        check_vma=False,
    )
```

profile of v0, /device:TPU:29, one launch (start us, length us, event | category | flops | bytes accessed | tf_op | source)
XLA Modules:
  0.0 179.2 jit_solution(12051949255293508783)
XLA Ops:
  0.6 1.1 slice.344
  2.5 16.0 %collective-permute-start = (f32[3,1,8,512]{3,2,1,0:T(8,128)S(1)}, f32[3,1,8,512]{3,2,1,0:T(8,128)S(1)}, u32[]{:S(2)}, u32[]{:S(2)}) collective-permute-start(f32[3,1,8,512]{3,2,1,0:T(8,128)S(1)} %get-tuple-element.75), channel_id=1, source_target_pairs={{0,32},{32,64},{64,96},{96,128},{128,160},{160,192},{192,224},{224... | collective-permute-start | bytes 147464 | tf_op jit(solution)/shard_map/ppermute | solution.py:27
  18.5 1.9 %collective-permute-start.1 = (f32[3,1,8,512]{3,2,1,0:T(8,128)S(1)}, f32[3,1,8,512]{3,2,1,0:T(8,128)S(1)}, u32[]{:S(2)}, u32[]{:S(2)}) collective-permute-start(f32[3,1,8,512]{3,2,1,0:T(8,128)S(1)} %get-tuple-element.76), channel_id=1, source_target_pairs={{32,0},{64,32},{96,64},{128,96},{160,128},{192,160},{224,192},{256... | collective-permute-start | bytes 147464 | tf_op jit(solution)/shard_map/ppermute | solution.py:30
  20.4 1.0 slice_bitcast_fusion.4
  21.4 12.0 %collective-permute-done.1 = f32[3,1,8,512]{3,2,1,0:T(8,128)S(1)} collective-permute-done((f32[3,1,8,512]{3,2,1,0:T(8,128)S(1)}, f32[3,1,8,512]{3,2,1,0:T(8,128)S(1)}, u32[]{:S(2)}, u32[]{:S(2)}) %collective-permute-start.1) | collective-permute-done | bytes 49184 | tf_op jit(solution)/shard_map/ppermute | solution.py:30
  33.5 1.9 %collective-permute-start.2 = (f32[3,18,1,512]{3,2,1,0:T(1,128)S(1)}, f32[3,18,1,512]{3,2,1,0:T(1,128)S(1)}, u32[]{:S(2)}, u32[]{:S(2)}) collective-permute-start(f32[3,18,1,512]{3,2,1,0:T(1,128)S(1)} %get-tuple-element.73), channel_id=1, source_target_pairs={{0,1},{1,2},{2,3},{3,4},{4,5},{5,6},{6,7},{7,8},{8,9},{9,10},{10,1... | collective-permute-start | bytes 331784 | tf_op jit(solution)/shard_map/ppermute | solution.py:27
  35.5 3.4 %collective-permute-start.3 = (f32[3,18,1,512]{3,2,1,0:T(1,128)S(1)}, f32[3,18,1,512]{3,2,1,0:T(1,128)S(1)}, u32[]{:S(2)}, u32[]{:S(2)}) collective-permute-start(f32[3,18,1,512]{3,2,1,0:T(1,128)S(1)} %get-tuple-element.74), channel_id=1, source_target_pairs={{1,0},{2,1},{3,2},{4,3},{5,4},{6,5},{7,6},{8,7},{9,8},{10,9},{11,1... | collective-permute-start | bytes 331784 | tf_op jit(solution)/shard_map/ppermute | solution.py:30
  39.0 4.0 %collective-permute-done.3 = f32[3,18,1,512]{3,2,1,0:T(1,128)S(1)} collective-permute-done((f32[3,18,1,512]{3,2,1,0:T(1,128)S(1)}, f32[3,18,1,512]{3,2,1,0:T(1,128)S(1)}, u32[]{:S(2)}, u32[]{:S(2)}) %collective-permute-start.3) | collective-permute-done | bytes 110624 | tf_op jit(solution)/shard_map/ppermute | solution.py:30
  43.3 1.3 multiply_bitcast_fusion.3
  45.3 1.2 copy-done.5
  46.8 3.8 %collective-permute-start.4 = (f32[4,1,8,512]{3,2,1,0:T(8,128)S(1)}, f32[4,1,8,512]{3,2,1,0:T(8,128)S(1)}, u32[]{:S(2)}, u32[]{:S(2)}) collective-permute-start(f32[4,1,8,512]{3,2,1,0:T(8,128)S(1)} %get-tuple-element.71), channel_id=1, source_target_pairs={{0,32},{32,64},{64,96},{96,128},{128,160},{160,192},{192,224},{224... | collective-permute-start | bytes 196616 | tf_op jit(solution)/shard_map/ppermute | solution.py:27
  50.6 1.9 %collective-permute-start.5 = (f32[4,1,8,512]{3,2,1,0:T(8,128)S(1)}, f32[4,1,8,512]{3,2,1,0:T(8,128)S(1)}, u32[]{:S(2)}, u32[]{:S(2)}) collective-permute-start(f32[4,1,8,512]{3,2,1,0:T(8,128)S(1)} %get-tuple-element.72), channel_id=1, source_target_pairs={{32,0},{64,32},{96,64},{128,96},{160,128},{192,160},{224,192},{256... | collective-permute-start | bytes 196616 | tf_op jit(solution)/shard_map/ppermute | solution.py:30
  53.2 13.8 %collective-permute-done.5 = f32[4,1,8,512]{3,2,1,0:T(8,128)S(1)} collective-permute-done((f32[4,1,8,512]{3,2,1,0:T(8,128)S(1)}, f32[4,1,8,512]{3,2,1,0:T(8,128)S(1)}, u32[]{:S(2)}, u32[]{:S(2)}) %collective-permute-start.5) | collective-permute-done | bytes 65568 | tf_op jit(solution)/shard_map/ppermute | solution.py:30
  67.1 1.9 %collective-permute-start.6 = (f32[4,18,1,512]{3,2,1,0:T(1,128)S(1)}, f32[4,18,1,512]{3,2,1,0:T(1,128)S(1)}, u32[]{:S(2)}, u32[]{:S(2)}) collective-permute-start(f32[4,18,1,512]{3,2,1,0:T(1,128)S(1)} %get-tuple-element.64), channel_id=1, source_target_pairs={{0,1},{1,2},{2,3},{3,4},{4,5},{5,6},{6,7},{7,8},{8,9},{9,10},{10,1... | collective-permute-start | bytes 442376 | tf_op jit(solution)/shard_map/ppermute | solution.py:27
  69.1 3.4 %collective-permute-start.7 = (f32[4,18,1,512]{3,2,1,0:T(1,128)S(1)}, f32[4,18,1,512]{3,2,1,0:T(1,128)S(1)}, u32[]{:S(2)}, u32[]{:S(2)}) collective-permute-start(f32[4,18,1,512]{3,2,1,0:T(1,128)S(1)} %get-tuple-element.63), channel_id=1, source_target_pairs={{1,0},{2,1},{3,2},{4,3},{5,4},{6,5},{7,6},{8,7},{9,8},{10,9},{11,1... | collective-permute-start | bytes 442376 | tf_op jit(solution)/shard_map/ppermute | solution.py:30
  73.0 4.0 %collective-permute-done.7 = f32[4,18,1,512]{3,2,1,0:T(1,128)S(1)} collective-permute-done((f32[4,18,1,512]{3,2,1,0:T(1,128)S(1)}, f32[4,18,1,512]{3,2,1,0:T(1,128)S(1)}, u32[]{:S(2)}, u32[]{:S(2)}) %collective-permute-start.7) | collective-permute-done | bytes 147488 | tf_op jit(solution)/shard_map/ppermute | solution.py:30
  81.2 2.8 %collective-permute-start.8 = (f32[4,1,8,512]{3,2,1,0:T(8,128)S(1)}, f32[4,1,8,512]{3,2,1,0:T(8,128)S(1)}, u32[]{:S(2)}, u32[]{:S(2)}) collective-permute-start(f32[4,1,8,512]{3,2,1,0:T(8,128)S(1)} %get-tuple-element.69), channel_id=1, source_target_pairs={{0,32},{32,64},{64,96},{96,128},{128,160},{160,192},{192,224},{224... | collective-permute-start | bytes 196616 | tf_op jit(solution)/shard_map/ppermute | solution.py:27
  84.0 1.9 %collective-permute-start.9 = (f32[4,1,8,512]{3,2,1,0:T(8,128)S(1)}, f32[4,1,8,512]{3,2,1,0:T(8,128)S(1)}, u32[]{:S(2)}, u32[]{:S(2)}) collective-permute-start(f32[4,1,8,512]{3,2,1,0:T(8,128)S(1)} %get-tuple-element.70), channel_id=1, source_target_pairs={{32,0},{64,32},{96,64},{128,96},{160,128},{192,160},{224,192},{256... | collective-permute-start | bytes 196616 | tf_op jit(solution)/shard_map/ppermute | solution.py:30
  86.2 13.5 %collective-permute-done.9 = f32[4,1,8,512]{3,2,1,0:T(8,128)S(1)} collective-permute-done((f32[4,1,8,512]{3,2,1,0:T(8,128)S(1)}, f32[4,1,8,512]{3,2,1,0:T(8,128)S(1)}, u32[]{:S(2)}, u32[]{:S(2)}) %collective-permute-start.9) | collective-permute-done | bytes 65568 | tf_op jit(solution)/shard_map/ppermute | solution.py:30
  99.7 0.9 pad_maximum_fusion.45
  100.6 1.9 %collective-permute-start.10 = (f32[4,18,1,512]{3,2,1,0:T(1,128)}, f32[4,18,1,512]{3,2,1,0:T(1,128)}, u32[]{:S(2)}, u32[]{:S(2)}) collective-permute-start(f32[4,18,1,512]{3,2,1,0:T(1,128)} %get-tuple-element.62), channel_id=1, source_target_pairs={{0,1},{1,2},{2,3},{3,4},{4,5},{5,6},{6,7},{7,8},{8,9},{9,10},{10,1... | collective-permute-start | bytes 442376 | tf_op jit(solution)/shard_map/ppermute | solution.py:27
  102.5 3.4 %collective-permute-start.11 = (f32[4,18,1,512]{3,2,1,0:T(1,128)}, f32[4,18,1,512]{3,2,1,0:T(1,128)}, u32[]{:S(2)}, u32[]{:S(2)}) collective-permute-start(f32[4,18,1,512]{3,2,1,0:T(1,128)} %get-tuple-element.61), channel_id=1, source_target_pairs={{1,0},{2,1},{3,2},{4,3},{5,4},{6,5},{7,6},{8,7},{9,8},{10,9},{11,1... | collective-permute-start | bytes 442376 | tf_op jit(solution)/shard_map/ppermute | solution.py:30
  106.5 1.2 multiply_reduce_fusion.1
  107.8 3.1 %collective-permute-done.11 = f32[4,18,1,512]{3,2,1,0:T(1,128)} collective-permute-done((f32[4,18,1,512]{3,2,1,0:T(1,128)}, f32[4,18,1,512]{3,2,1,0:T(1,128)}, u32[]{:S(2)}, u32[]{:S(2)}) %collective-permute-start.11) | collective-permute-done | bytes 147488 | tf_op jit(solution)/shard_map/ppermute | solution.py:30
  114.7 2.0 %fusion.26 = f32[3,16,8,512]{3,2,1,0:T(8,128)S(1)} fusion(f32[3,16,8,512]{3,2,1,0:T(8,128)S(1)} %slice-done, f32[4,18,1,512]{3,2,1,0:T(1,128)} %collective-permute-done.10, f32[4,1,8,512]{3,2,1,0:T(8,128)S(1)} %collective-permute-done.9, f32[4,16,8,512]{3,2,1,0:T(8,128)S(1)} %copy-done.2, f32[4,1,8,512]{3,2,1,0:T(8,128)S(1)} %collective-permute-done.8, ...), kind=kLoop, calls=%fused_computation.44 | loop fusion | flops 6094848 | bytes 5406720 | tf_op jit(solution)/shard_map/add | solution.py:79
  117.5 2.6 %collective-permute-start.12 = (f32[4,1,8,512]{3,2,1,0:T(8,128)S(1)}, f32[4,1,8,512]{3,2,1,0:T(8,128)S(1)}, u32[]{:S(2)}, u32[]{:S(2)}) collective-permute-start(f32[4,1,8,512]{3,2,1,0:T(8,128)S(1)} %get-tuple-element.67), channel_id=1, source_target_pairs={{0,32},{32,64},{64,96},{96,128},{128,160},{160,192},{192,224},{224... | collective-permute-start | bytes 196616 | tf_op jit(solution)/shard_map/ppermute | solution.py:27
  120.1 1.9 %collective-permute-start.13 = (f32[4,1,8,512]{3,2,1,0:T(8,128)S(1)}, f32[4,1,8,512]{3,2,1,0:T(8,128)S(1)}, u32[]{:S(2)}, u32[]{:S(2)}) collective-permute-start(f32[4,1,8,512]{3,2,1,0:T(8,128)S(1)} %get-tuple-element.68), channel_id=1, source_target_pairs={{32,0},{64,32},{96,64},{128,96},{160,128},{192,160},{224,192},{256... | collective-permute-start | bytes 196616 | tf_op jit(solution)/shard_map/ppermute | solution.py:30
  122.8 13.5 %collective-permute-done.13 = f32[4,1,8,512]{3,2,1,0:T(8,128)S(1)} collective-permute-done((f32[4,1,8,512]{3,2,1,0:T(8,128)S(1)}, f32[4,1,8,512]{3,2,1,0:T(8,128)S(1)}, u32[]{:S(2)}, u32[]{:S(2)}) %collective-permute-start.13) | collective-permute-done | bytes 65568 | tf_op jit(solution)/shard_map/ppermute | solution.py:30
  136.4 2.0 %collective-permute-start.14 = (f32[4,18,1,512]{3,2,1,0:T(1,128)S(1)}, f32[4,18,1,512]{3,2,1,0:T(1,128)S(1)}, u32[]{:S(2)}, u32[]{:S(2)}) collective-permute-start(f32[4,18,1,512]{3,2,1,0:T(1,128)S(1)} %get-tuple-element.60), channel_id=1, source_target_pairs={{0,1},{1,2},{2,3},{3,4},{4,5},{5,6},{6,7},{7,8},{8,9},{9,10},{10,1... | collective-permute-start | bytes 442376 | tf_op jit(solution)/shard_map/ppermute | solution.py:27
  138.4 3.5 %collective-permute-start.15 = (f32[4,18,1,512]{3,2,1,0:T(1,128)S(1)}, f32[4,18,1,512]{3,2,1,0:T(1,128)S(1)}, u32[]{:S(2)}, u32[]{:S(2)}) collective-permute-start(f32[4,18,1,512]{3,2,1,0:T(1,128)S(1)} %get-tuple-element.59), channel_id=1, source_target_pairs={{1,0},{2,1},{3,2},{4,3},{5,4},{6,5},{7,6},{8,7},{9,8},{10,9},{11,1... | collective-permute-start | bytes 442376 | tf_op jit(solution)/shard_map/ppermute | solution.py:30
  142.3 4.1 %collective-permute-done.15 = f32[4,18,1,512]{3,2,1,0:T(1,128)S(1)} collective-permute-done((f32[4,18,1,512]{3,2,1,0:T(1,128)S(1)}, f32[4,18,1,512]{3,2,1,0:T(1,128)S(1)}, u32[]{:S(2)}, u32[]{:S(2)}) %collective-permute-start.15) | collective-permute-done | bytes 147488 | tf_op jit(solution)/shard_map/ppermute | solution.py:30
  149.9 28.4 %while.10 = (s32[]{:T(128)}, f32[3,16,8,512]{3,2,1,0:T(8,128)S(1)}, s32[]{:T(128)}, f32[3,16,8,512]{3,2,1,0:T(8,128)S(1)}, f32[3,16,8,512]{3,2,1,0:T(8,128)S(1)}, /*index=5*/s32[]{:T(128)}) while((s32[]{:T(128)}, f32[3,16,8,512]{3,2,1,0:T(8,128)S(1)}, s32[]{:T(128)}, f32[3,16,8,512]{3,2,1,0:T(8,128)S(1)}, f32[3,16,8,512]{3,2,1,0:T(8,128)S(1)}, ...), condition=%wide.region_4.5_spmd, body=%wide.region_2.4_spmd.sunk | while | flops 1376258 | bytes 5767237 | solution.py:115
  (221 shorter events, 45.1 us)
Async XLA Ops:
  0.6 32.8 %copy-start.17 = (f32[16,8,512]{2,1,0:T(8,128)S(1)}, f32[16,8,512]{2,1,0:T(8,128)}, u32[]{:S(2)}) copy-start(f32[16,8,512]{2,1,0:T(8,128)} %param.7) | copy-start | bytes 786436
  2.5 18.9 %collective-permute-start = (f32[3,1,8,512]{3,2,1,0:T(8,128)S(1)}, f32[3,1,8,512]{3,2,1,0:T(8,128)S(1)}, u32[]{:S(2)}, u32[]{:S(2)}) collective-permute-start(f32[3,1,8,512]{3,2,1,0:T(8,128)S(1)} %get-tuple-element.75), channel_id=1, source_target_pairs={{0,32},{32,64},{64,96},{96,128},{128,160},{160,192},{192,224},{224... | collective-permute-start | bytes 147464 | tf_op jit(solution)/shard_map/ppermute | solution.py:27
  18.5 14.9 %collective-permute-start.1 = (f32[3,1,8,512]{3,2,1,0:T(8,128)S(1)}, f32[3,1,8,512]{3,2,1,0:T(8,128)S(1)}, u32[]{:S(2)}, u32[]{:S(2)}) collective-permute-start(f32[3,1,8,512]{3,2,1,0:T(8,128)S(1)} %get-tuple-element.76), channel_id=1, source_target_pairs={{32,0},{64,32},{96,64},{128,96},{160,128},{192,160},{224,192},{256... | collective-permute-start | bytes 147464 | tf_op jit(solution)/shard_map/ppermute | solution.py:30
  33.5 5.5 %collective-permute-start.2 = (f32[3,18,1,512]{3,2,1,0:T(1,128)S(1)}, f32[3,18,1,512]{3,2,1,0:T(1,128)S(1)}, u32[]{:S(2)}, u32[]{:S(2)}) collective-permute-start(f32[3,18,1,512]{3,2,1,0:T(1,128)S(1)} %get-tuple-element.73), channel_id=1, source_target_pairs={{0,1},{1,2},{2,3},{3,4},{4,5},{5,6},{6,7},{7,8},{8,9},{9,10},{10,1... | collective-permute-start | bytes 331784 | tf_op jit(solution)/shard_map/ppermute | solution.py:27
  35.5 7.6 %collective-permute-start.3 = (f32[3,18,1,512]{3,2,1,0:T(1,128)S(1)}, f32[3,18,1,512]{3,2,1,0:T(1,128)S(1)}, u32[]{:S(2)}, u32[]{:S(2)}) collective-permute-start(f32[3,18,1,512]{3,2,1,0:T(1,128)S(1)} %get-tuple-element.74), channel_id=1, source_target_pairs={{1,0},{2,1},{3,2},{4,3},{5,4},{6,5},{7,6},{8,7},{9,8},{10,9},{11,1... | collective-permute-start | bytes 331784 | tf_op jit(solution)/shard_map/ppermute | solution.py:30
  44.6 33.7 %copy-start.18 = (f32[16,8,512]{2,1,0:T(8,128)}, f32[16,8,512]{2,1,0:T(8,128)S(1)}, u32[]{:S(2)}) copy-start(f32[16,8,512]{2,1,0:T(8,128)S(1)} %get-tuple-element.80) | copy-start | bytes 786436
  44.6 33.7 %copy-start.20 = (f32[16,8,512]{2,1,0:T(8,128)}, f32[16,8,512]{2,1,0:T(8,128)S(1)}, u32[]{:S(2)}) copy-start(f32[16,8,512]{2,1,0:T(8,128)S(1)} %get-tuple-element.81) | copy-start | bytes 786436
  44.6 33.7 %copy-start.22 = (f32[16,8,512]{2,1,0:T(8,128)}, f32[16,8,512]{2,1,0:T(8,128)S(1)}, u32[]{:S(2)}) copy-start(f32[16,8,512]{2,1,0:T(8,128)S(1)} %get-tuple-element.82) | copy-start | bytes 786436
  44.6 33.7 %copy-start.24 = (f32[16,8,512]{2,1,0:T(8,128)}, f32[16,8,512]{2,1,0:T(8,128)S(1)}, u32[]{:S(2)}) copy-start(f32[16,8,512]{2,1,0:T(8,128)S(1)} %get-tuple-element.83) | copy-start | bytes 786436
  44.6 33.7 %copy-start.26 = (f32[16,8,512]{2,1,0:T(8,128)}, f32[16,8,512]{2,1,0:T(8,128)S(1)}, u32[]{:S(2)}) copy-start(f32[16,8,512]{2,1,0:T(8,128)S(1)} %get-tuple-element.84) | copy-start | bytes 786436
  44.6 33.7 %copy-start.28 = (f32[16,8,512]{2,1,0:T(8,128)}, f32[16,8,512]{2,1,0:T(8,128)S(1)}, u32[]{:S(2)}) copy-start(f32[16,8,512]{2,1,0:T(8,128)S(1)} %get-tuple-element.85) | copy-start | bytes 786436
  44.6 35.6 %copy-start.9 = (f32[1,16,8,512]{3,2,1,0:T(8,128)}, f32[1,16,8,512]{3,2,1,0:T(8,128)S(1)}, u32[]{:S(2)}) copy-start(f32[1,16,8,512]{3,2,1,0:T(8,128)S(1)} %get-tuple-element.79) | copy-start | bytes 786436
  45.3 32.0 %copy-start.13 = (f32[16,8,512]{2,1,0:T(8,128)}, f32[16,8,512]{2,1,0:T(8,128)S(1)}, u32[]{:S(2)}) copy-start(f32[16,8,512]{2,1,0:T(8,128)S(1)} %fusion.40) | copy-start | bytes 786436
  45.3 34.9 %copy-start.11 = (f32[1,16,8,512]{3,2,1,0:T(8,128)}, f32[1,16,8,512]{3,2,1,0:T(8,128)S(1)}, u32[]{:S(2)}) copy-start(f32[1,16,8,512]{3,2,1,0:T(8,128)S(1)} %divide_bitcast_fusion.1) | copy-start | bytes 786436
  46.7 30.4 %copy-start.3 = (f32[4,16,8,512]{3,2,1,0:T(8,128)}, f32[4,16,8,512]{3,2,1,0:T(8,128)S(1)}, u32[]{:S(2)}) copy-start(f32[4,16,8,512]{3,2,1,0:T(8,128)S(1)} %fusion.79) | copy-start | bytes 3145732
  46.8 6.4 %collective-permute-start.4 = (f32[4,1,8,512]{3,2,1,0:T(8,128)S(1)}, f32[4,1,8,512]{3,2,1,0:T(8,128)S(1)}, u32[]{:S(2)}, u32[]{:S(2)}) collective-permute-start(f32[4,1,8,512]{3,2,1,0:T(8,128)S(1)} %get-tuple-element.71), channel_id=1, source_target_pairs={{0,32},{32,64},{64,96},{96,128},{128,160},{160,192},{192,224},{224... | collective-permute-start | bytes 196616 | tf_op jit(solution)/shard_map/ppermute | solution.py:27
  50.6 16.3 %collective-permute-start.5 = (f32[4,1,8,512]{3,2,1,0:T(8,128)S(1)}, f32[4,1,8,512]{3,2,1,0:T(8,128)S(1)}, u32[]{:S(2)}, u32[]{:S(2)}) collective-permute-start(f32[4,1,8,512]{3,2,1,0:T(8,128)S(1)} %get-tuple-element.72), channel_id=1, source_target_pairs={{32,0},{64,32},{96,64},{128,96},{160,128},{192,160},{224,192},{256... | collective-permute-start | bytes 196616 | tf_op jit(solution)/shard_map/ppermute | solution.py:30
  67.1 5.9 %collective-permute-start.6 = (f32[4,18,1,512]{3,2,1,0:T(1,128)S(1)}, f32[4,18,1,512]{3,2,1,0:T(1,128)S(1)}, u32[]{:S(2)}, u32[]{:S(2)}) collective-permute-start(f32[4,18,1,512]{3,2,1,0:T(1,128)S(1)} %get-tuple-element.64), channel_id=1, source_target_pairs={{0,1},{1,2},{2,3},{3,4},{4,5},{5,6},{6,7},{7,8},{8,9},{9,10},{10,1... | collective-permute-start | bytes 442376 | tf_op jit(solution)/shard_map/ppermute | solution.py:27
  69.1 8.0 %collective-permute-start.7 = (f32[4,18,1,512]{3,2,1,0:T(1,128)S(1)}, f32[4,18,1,512]{3,2,1,0:T(1,128)S(1)}, u32[]{:S(2)}, u32[]{:S(2)}) collective-permute-start(f32[4,18,1,512]{3,2,1,0:T(1,128)S(1)} %get-tuple-element.63), channel_id=1, source_target_pairs={{1,0},{2,1},{3,2},{4,3},{5,4},{6,5},{7,6},{8,7},{9,8},{10,9},{11,1... | collective-permute-start | bytes 442376 | tf_op jit(solution)/shard_map/ppermute | solution.py:30
  77.5 2.8 %copy-start.33 = (f32[1,16,8,512]{3,2,1,0:T(8,128)}, f32[1,16,8,512]{3,2,1,0:T(8,128)S(1)}, u32[]{:S(2)}) copy-start(f32[1,16,8,512]{3,2,1,0:T(8,128)S(1)} %fusion.85) | copy-start | bytes 786436
  81.2 29.7 %copy-start.1 = (f32[4,16,8,512]{3,2,1,0:T(8,128)}, f32[4,16,8,512]{3,2,1,0:T(8,128)S(1)}, u32[]{:S(2)}) copy-start(f32[4,16,8,512]{3,2,1,0:T(8,128)S(1)} %fusion.78) | copy-start | bytes 3145732
  81.2 5.0 %collective-permute-start.8 = (f32[4,1,8,512]{3,2,1,0:T(8,128)S(1)}, f32[4,1,8,512]{3,2,1,0:T(8,128)S(1)}, u32[]{:S(2)}, u32[]{:S(2)}) collective-permute-start(f32[4,1,8,512]{3,2,1,0:T(8,128)S(1)} %get-tuple-element.69), channel_id=1, source_target_pairs={{0,32},{32,64},{64,96},{96,128},{128,160},{160,192},{192,224},{224... | collective-permute-start | bytes 196616 | tf_op jit(solution)/shard_map/ppermute | solution.py:27
  84.0 15.7 %collective-permute-start.9 = (f32[4,1,8,512]{3,2,1,0:T(8,128)S(1)}, f32[4,1,8,512]{3,2,1,0:T(8,128)S(1)}, u32[]{:S(2)}, u32[]{:S(2)}) collective-permute-start(f32[4,1,8,512]{3,2,1,0:T(8,128)S(1)} %get-tuple-element.70), channel_id=1, source_target_pairs={{32,0},{64,32},{96,64},{128,96},{160,128},{192,160},{224,192},{256... | collective-permute-start | bytes 196616 | tf_op jit(solution)/shard_map/ppermute | solution.py:30
  100.6 7.2 %collective-permute-start.10 = (f32[4,18,1,512]{3,2,1,0:T(1,128)}, f32[4,18,1,512]{3,2,1,0:T(1,128)}, u32[]{:S(2)}, u32[]{:S(2)}) collective-permute-start(f32[4,18,1,512]{3,2,1,0:T(1,128)} %get-tuple-element.62), channel_id=1, source_target_pairs={{0,1},{1,2},{2,3},{3,4},{4,5},{5,6},{6,7},{7,8},{8,9},{9,10},{10,1... | collective-permute-start | bytes 442376 | tf_op jit(solution)/shard_map/ppermute | solution.py:27
  102.5 8.3 %collective-permute-start.11 = (f32[4,18,1,512]{3,2,1,0:T(1,128)}, f32[4,18,1,512]{3,2,1,0:T(1,128)}, u32[]{:S(2)}, u32[]{:S(2)}) collective-permute-start(f32[4,18,1,512]{3,2,1,0:T(1,128)} %get-tuple-element.61), channel_id=1, source_target_pairs={{1,0},{2,1},{3,2},{4,3},{5,4},{6,5},{7,6},{8,7},{9,8},{10,9},{11,1... | collective-permute-start | bytes 442376 | tf_op jit(solution)/shard_map/ppermute | solution.py:30
  117.4 24.5 %copy-start.30 = (f32[1,16,8,512]{3,2,1,0:T(8,128)S(1)}, f32[1,16,8,512]{3,2,1,0:T(8,128)}, u32[]{:S(2)}) copy-start(f32[1,16,8,512]{3,2,1,0:T(8,128)} %get-tuple-element.77) | copy-start | bytes 786436
  117.5 24.5 %copy-start.31 = (f32[1,16,8,512]{3,2,1,0:T(8,128)S(1)}, f32[1,16,8,512]{3,2,1,0:T(8,128)}, u32[]{:S(2)}) copy-start(f32[1,16,8,512]{3,2,1,0:T(8,128)} %get-tuple-element.78) | copy-start | bytes 786436
  117.5 24.5 %copy-start.32 = (f32[1,16,8,512]{3,2,1,0:T(8,128)S(1)}, f32[1,16,8,512]{3,2,1,0:T(8,128)}, u32[]{:S(2)}) copy-start(f32[1,16,8,512]{3,2,1,0:T(8,128)} %get-tuple-element.86) | copy-start | bytes 786436
  117.5 5.3 %collective-permute-start.12 = (f32[4,1,8,512]{3,2,1,0:T(8,128)S(1)}, f32[4,1,8,512]{3,2,1,0:T(8,128)S(1)}, u32[]{:S(2)}, u32[]{:S(2)}) collective-permute-start(f32[4,1,8,512]{3,2,1,0:T(8,128)S(1)} %get-tuple-element.67), channel_id=1, source_target_pairs={{0,32},{32,64},{64,96},{96,128},{128,160},{160,192},{192,224},{224... | collective-permute-start | bytes 196616 | tf_op jit(solution)/shard_map/ppermute | solution.py:27
  120.1 16.1 %collective-permute-start.13 = (f32[4,1,8,512]{3,2,1,0:T(8,128)S(1)}, f32[4,1,8,512]{3,2,1,0:T(8,128)S(1)}, u32[]{:S(2)}, u32[]{:S(2)}) collective-permute-start(f32[4,1,8,512]{3,2,1,0:T(8,128)S(1)} %get-tuple-element.68), channel_id=1, source_target_pairs={{32,0},{64,32},{96,64},{128,96},{160,128},{192,160},{224,192},{256... | collective-permute-start | bytes 196616 | tf_op jit(solution)/shard_map/ppermute | solution.py:30
  136.4 5.9 %collective-permute-start.14 = (f32[4,18,1,512]{3,2,1,0:T(1,128)S(1)}, f32[4,18,1,512]{3,2,1,0:T(1,128)S(1)}, u32[]{:S(2)}, u32[]{:S(2)}) collective-permute-start(f32[4,18,1,512]{3,2,1,0:T(1,128)S(1)} %get-tuple-element.60), channel_id=1, source_target_pairs={{0,1},{1,2},{2,3},{3,4},{4,5},{5,6},{6,7},{7,8},{8,9},{9,10},{10,1... | collective-permute-start | bytes 442376 | tf_op jit(solution)/shard_map/ppermute | solution.py:27
  138.4 8.0 %collective-permute-start.15 = (f32[4,18,1,512]{3,2,1,0:T(1,128)S(1)}, f32[4,18,1,512]{3,2,1,0:T(1,128)S(1)}, u32[]{:S(2)}, u32[]{:S(2)}) collective-permute-start(f32[4,18,1,512]{3,2,1,0:T(1,128)S(1)} %get-tuple-element.59), channel_id=1, source_target_pairs={{1,0},{2,1},{3,2},{4,3},{5,4},{6,5},{7,6},{8,7},{9,8},{10,9},{11,1... | collective-permute-start | bytes 442376 | tf_op jit(solution)/shard_map/ppermute | solution.py:30
  (21 other events, 31.8 us)
where the time goes:
time: 180 us; the launch traced here: 179 us
  waiting for transfers between devices  70.4 us (39%)
  starting transfers between devices  54.2 us (30%)
  other arithmetic  42.4 us (24%)
  local copies, waits for them, and re-layouts  9 us (5%)
  between operations  2.05 us (1%)
    ppermute x8, waiting for transfers between devices, padded_2(): lax.ppermute(lax.slice_in_dim(block, 0, width, axis=dim), axis, backward)  68 us
    ppermute x8, starting transfers between devices, padded_2(): lax.ppermute(lax.slice_in_dim(block, block.shape[dim] - width, None, axis...  33 us
    add x32, other arithmetic, relax_once(): relaxed + RELAX_STEP / RELAX_INNER * (target - relaxed - NORMAL_WEIGHT *...  21.8 us
    ppermute x8, starting transfers between devices, padded_2(): lax.ppermute(lax.slice_in_dim(block, 0, width, axis=dim), axis, backward)  21.2 us
    unnamed x71, local copies, waits for them, and re-layouts  5.22 us
    reduce_sum x32, other arithmetic, relax_once(): along = jnp.sum(normal * relaxed, axis=0, keepdims=True)  4.9 us
    add x3, other arithmetic, operate(): return jnp.concatenate([damage_part[None], disp_part + transfer], axis=0)  3.81 us
  transfers between devices with their start and end apart: 16, of which 14 were waited for; matrix products, arithmetic and copies ran while one was open for 1% of the time, Pallas kernels for 0%

commit v1 on v0

--- a/solution.py
+++ b/solution.py
@@ -19,17 +19,31 @@
 NORMAL_FLOOR = 0.05
 
 
-def padded_2(block, sides, width):
-    for axis, dim in sides:
-        count = lax.axis_size(axis)
-        forward = [(i, i + 1) for i in range(count - 1)]
-        backward = [(target, source) for source, target in forward]
-        low = lax.ppermute(
-            lax.slice_in_dim(block, block.shape[dim] - width, None, axis=dim), axis, forward
-        )
-        high = lax.ppermute(lax.slice_in_dim(block, 0, width, axis=dim), axis, backward)
-        block = jnp.concatenate([low, block, high], axis=dim)
-    return block
+def neighbours(block, axis, dim):
+    count = lax.axis_size(axis)
+    forward = [(i, i + 1) for i in range(count - 1)]
+    backward = [(target, source) for source, target in forward]
+    width = block.shape[dim]
+    low = lax.ppermute(lax.slice_in_dim(block, width - 1, None, axis=dim), axis, forward)
+    high = lax.ppermute(lax.slice_in_dim(block, 0, 1, axis=dim), axis, backward)
+    return low, high
+
+
+def frame(block, xs, ys):
+    lead = block.ndim - 3
+    xlo, xhi = xs
+    ylo, yhi = ys
+    mid = jnp.concatenate([xlo, block, xhi], axis=lead)
+    widths = [(0, 0)] * lead + [(1, 1), (0, 0), (0, 0)]
+    ylo = jnp.pad(ylo, widths)
+    yhi = jnp.pad(yhi, widths)
+    return jnp.concatenate([ylo, mid, yhi], axis=lead + 1)
+
+
+def framed_state(state):
+    xs = neighbours(state, "gx", 1)
+    ys = neighbours(state, "gy", 2)
+    return frame(state, xs, ys)
 
 
 def shifted(field):
@@ -79,16 +93,16 @@
     return jnp.concatenate([damage_part[None], disp_part + transfer], axis=0)
 
 
-def chebyshev(faces, energy, coupling, inverse, source, widen, keep):
+def chebyshev(faces, energy, coupling, inverse, source, widen):
     ratio = CENTER_VALUE / HALF_WIDTH
     rho = 1.0 / ratio
     update = inverse * source / CENTER_VALUE
-    state = keep(update)
+    state = update
     for sweep in range(SWEEPS):
         residual = source - operate(faces, energy, coupling, widen(state))
         rho_next = 1.0 / (2.0 * ratio - rho)
         update = rho_next * rho * update + 2.0 * rho_next / HALF_WIDTH * inverse * residual
-        state = keep(state + update)
+        state = state + update
         rho = rho_next
     return state
 
@@ -102,38 +116,39 @@
     return grad / length
 
 
-def relax_once(target, normal, relaxed):
-    along = jnp.sum(normal * relaxed, axis=0, keepdims=True)
-    return relaxed + RELAX_STEP / RELAX_INNER * (target - relaxed - NORMAL_WEIGHT * along * normal)
-
-
 def relax(target, normal, count):
-
-    def advance(level, relaxed):
-        return relax_once(target, normal, relaxed)
-
-    return lax.fori_loop(0, count * RELAX_INNER, advance, target)
-
-
-def unchanged(state):
-    return state
+    step = RELAX_STEP / RELAX_INNER
+    size = jnp.sum(normal * normal, axis=0, keepdims=True)
+    along = jnp.sum(normal * target, axis=0, keepdims=True)
+    factor = 1.0 - step * (1.0 + NORMAL_WEIGHT * size)
+    power = factor
+    for _ in range(3):
+        power = power * power
+    base = power
+    total = power
+    for level in range(2, 5):
+        total = jnp.where(count >= level, total * base, total)
+    gain = NORMAL_WEIGHT * (1.0 - total) / (1.0 + NORMAL_WEIGHT * size)
+    return target - (gain * along) * normal
 
 
 def body(damage, strain, seed_damage, seed_disp, brick_work):
-    framed = padded_2(jnp.stack([damage, strain[0], strain[1]]), (("gx", 1), ("gy", 2)), 1)
-    framed_damage = framed[0]
-    framed_strain = jnp.stack([framed[1], framed[2], jnp.pad(strain[2], ((1, 1), (1, 1), (0, 0)))])
+    pair_x = jnp.stack([damage, strain[0]])
+    pair_y = jnp.stack([damage, strain[1]])
+    xlo, xhi = neighbours(pair_x, "gx", 1)
+    ylo, yhi = neighbours(pair_y, "gy", 2)
+    framed_damage = frame(damage, (xlo[0], xhi[0]), (ylo[0], yhi[0]))
+    zero_x = jnp.zeros_like(xlo[1])
+    zero_y = jnp.zeros_like(ylo[1])
+    strain_x = frame(strain[0], (xlo[1], xhi[1]), (zero_y, zero_y))
+    strain_y = frame(strain[1], (zero_x, zero_x), (ylo[1], yhi[1]))
+    strain_z = jnp.pad(strain[2], ((1, 1), (1, 1), (0, 0)))
+    framed_strain = jnp.stack([strain_x, strain_y, strain_z])
     faces, energy, coupling, inverse = prepare(framed_damage, framed_strain)
     source = jnp.concatenate([seed_damage[None], seed_disp], axis=0)
-
-    def widen_faces(state):
-        return padded_2(state, (("gx", 1), ("gy", 2)), 1)
-
-    state = chebyshev(faces, energy, coupling, inverse, source, widen_faces, unchanged)
+    state = chebyshev(faces, energy, coupling, inverse, source, framed_state)
     normal = crack_normal(framed_damage)
-    target = state[1:]
-    own = brick_work[0, 0]
-    corrected = relax(target, normal, own)
+    corrected = relax(state[1:], normal, brick_work[0, 0])
     return (state[0], corrected)
 
 

time: 180 us -> 139 us (0.77)
  the two profiles are of different devices: /device:TPU:29 before, /device:TPU:33 now
where the time goes in v1:
time: 139 us; the launch traced here: 138 us
  starting transfers between devices  81.5 us (59%)
  waiting for transfers between devices  37.8 us (27%)
  other arithmetic  10.9 us (8%)
  local copies, waits for them, and re-layouts  6.06 us (4%)
  between operations  1.99 us (1%)
    ppermute x8, starting transfers between devices, neighbours(): lax.ppermute(lax.slice_in_dim(block, width - 1, None, axis=dim), axis, fo...  53 us
    ppermute x8, waiting for transfers between devices, neighbours(): high = lax.ppermute(lax.slice_in_dim(block, 0, 1, axis=dim), axis, backward)  37.1 us
    ppermute x8, starting transfers between devices, neighbours(): high = lax.ppermute(lax.slice_in_dim(block, 0, 1, axis=dim), axis, backward)  28.5 us
  transfers between devices with their start and end apart: 16, of which 4 were waited for; matrix products, arithmetic and copies ran while one was open for 1% of the time, Pallas kernels for 0%

profile of v1, /device:TPU:33, one launch (start us, length us, event | category | flops | bytes accessed | tf_op | source)
XLA Modules:
  0.0 138.3 jit_solution(10341000486361931716)
XLA Ops:
  0.6 1.2 slice_bitcast_fusion.14
  2.0 3.2 %collective-permute-start.2 = (f32[2,16,1,512]{3,2,1,0:T(1,128)S(1)}, f32[2,16,1,512]{3,2,1,0:T(1,128)S(1)}, u32[]{:S(2)}, u32[]{:S(2)}) collective-permute-start(f32[2,16,1,512]{3,2,1,0:T(1,128)S(1)} %get-tuple-element.39), channel_id=1, source_target_pairs={{0,1},{1,2},{2,3},{3,4},{4,5},{5,6},{6,7},{7,8},{8,9},{9,10},{10,1... | collective-permute-start | bytes 196616 | tf_op jit(solution)/shard_map/ppermute | solution.py:27
  5.2 4.2 %collective-permute-start.3 = (f32[2,16,1,512]{3,2,1,0:T(1,128)S(1)}, f32[2,16,1,512]{3,2,1,0:T(1,128)S(1)}, u32[]{:S(2)}, u32[]{:S(2)}) collective-permute-start(f32[2,16,1,512]{3,2,1,0:T(1,128)S(1)} %get-tuple-element.40), channel_id=1, source_target_pairs={{1,0},{2,1},{3,2},{4,3},{5,4},{6,5},{7,6},{8,7},{9,8},{10,9},{11,1... | collective-permute-start | bytes 196616 | tf_op jit(solution)/shard_map/ppermute | solution.py:28
  9.4 15.7 %collective-permute-start = (f32[2,1,8,512]{3,2,1,0:T(8,128)S(1)}, f32[2,1,8,512]{3,2,1,0:T(8,128)S(1)}, u32[]{:S(2)}, u32[]{:S(2)}) collective-permute-start(f32[2,1,8,512]{3,2,1,0:T(8,128)S(1)} %get-tuple-element.42), channel_id=1, source_target_pairs={{0,32},{32,64},{64,96},{96,128},{128,160},{160,192},{192,224},{224... | collective-permute-start | bytes 98312 | tf_op jit(solution)/shard_map/ppermute | solution.py:27
  25.1 1.9 %collective-permute-start.1 = (f32[2,1,8,512]{3,2,1,0:T(8,128)S(1)}, f32[2,1,8,512]{3,2,1,0:T(8,128)S(1)}, u32[]{:S(2)}, u32[]{:S(2)}) collective-permute-start(f32[2,1,8,512]{3,2,1,0:T(8,128)S(1)} %get-tuple-element.41), channel_id=1, source_target_pairs={{32,0},{64,32},{96,64},{128,96},{160,128},{192,160},{224,192},{256... | collective-permute-start | bytes 98312 | tf_op jit(solution)/shard_map/ppermute | solution.py:28
  27.9 11.2 %collective-permute-done.1 = f32[2,1,8,512]{3,2,1,0:T(8,128)S(1)} collective-permute-done((f32[2,1,8,512]{3,2,1,0:T(8,128)S(1)}, f32[2,1,8,512]{3,2,1,0:T(8,128)S(1)}, u32[]{:S(2)}, u32[]{:S(2)}) %collective-permute-start.1) | collective-permute-done | bytes 32800 | tf_op jit(solution)/shard_map/ppermute | solution.py:28
  40.1 0.5 divide_bitcast_fusion
  41.3 1.9 %collective-permute-start.4 = (f32[4,16,1,512]{3,2,1,0:T(1,128)S(1)}, f32[4,16,1,512]{3,2,1,0:T(1,128)S(1)}, u32[]{:S(2)}, u32[]{:S(2)}) collective-permute-start(f32[4,16,1,512]{3,2,1,0:T(1,128)S(1)} %get-tuple-element.31), channel_id=1, source_target_pairs={{0,1},{1,2},{2,3},{3,4},{4,5},{5,6},{6,7},{7,8},{8,9},{9,10},{10,1... | collective-permute-start | bytes 393224 | tf_op jit(solution)/shard_map/ppermute | solution.py:27
  43.2 5.5 %collective-permute-start.7 = (f32[4,16,1,512]{3,2,1,0:T(1,128)S(1)}, f32[4,16,1,512]{3,2,1,0:T(1,128)S(1)}, u32[]{:S(2)}, u32[]{:S(2)}) collective-permute-start(f32[4,16,1,512]{3,2,1,0:T(1,128)S(1)} %get-tuple-element.30), channel_id=1, source_target_pairs={{1,0},{2,1},{3,2},{4,3},{5,4},{6,5},{7,6},{8,7},{9,8},{10,9},{11,1... | collective-permute-start | bytes 393224 | tf_op jit(solution)/shard_map/ppermute | solution.py:28
  48.7 2.5 %collective-permute-start.5 = (f32[4,1,8,512]{3,2,1,0:T(8,128)S(1)}, f32[4,1,8,512]{3,2,1,0:T(8,128)S(1)}, u32[]{:S(2)}, u32[]{:S(2)}) collective-permute-start(f32[4,1,8,512]{3,2,1,0:T(8,128)S(1)} %get-tuple-element.32), channel_id=1, source_target_pairs={{0,32},{32,64},{64,96},{96,128},{128,160},{160,192},{192,224},{224... | collective-permute-start | bytes 196616 | tf_op jit(solution)/shard_map/ppermute | solution.py:27
  51.2 1.9 %collective-permute-start.6 = (f32[4,1,8,512]{3,2,1,0:T(8,128)S(1)}, f32[4,1,8,512]{3,2,1,0:T(8,128)S(1)}, u32[]{:S(2)}, u32[]{:S(2)}) collective-permute-start(f32[4,1,8,512]{3,2,1,0:T(8,128)S(1)} %get-tuple-element.33), channel_id=1, source_target_pairs={{32,0},{64,32},{96,64},{128,96},{160,128},{192,160},{224,192},{256... | collective-permute-start | bytes 196616 | tf_op jit(solution)/shard_map/ppermute | solution.py:28
  53.5 12.0 %collective-permute-done.6 = f32[4,1,8,512]{3,2,1,0:T(8,128)S(1)} collective-permute-done((f32[4,1,8,512]{3,2,1,0:T(8,128)S(1)}, f32[4,1,8,512]{3,2,1,0:T(8,128)S(1)}, u32[]{:S(2)}, u32[]{:S(2)}) %collective-permute-start.6) | collective-permute-done | bytes 65568 | tf_op jit(solution)/shard_map/ppermute | solution.py:28
  66.6 0.8 copy-done.3
  67.7 0.9 fusion.13
  69.1 1.9 %collective-permute-start.8 = (f32[4,16,1,512]{3,2,1,0:T(1,128)S(1)}, f32[4,16,1,512]{3,2,1,0:T(1,128)S(1)}, u32[]{:S(2)}, u32[]{:S(2)}) collective-permute-start(f32[4,16,1,512]{3,2,1,0:T(1,128)S(1)} %get-tuple-element.27), channel_id=1, source_target_pairs={{0,1},{1,2},{2,3},{3,4},{4,5},{5,6},{6,7},{7,8},{8,9},{9,10},{10,1... | collective-permute-start | bytes 393224 | tf_op jit(solution)/shard_map/ppermute | solution.py:27
  71.0 5.5 %collective-permute-start.11 = (f32[4,16,1,512]{3,2,1,0:T(1,128)S(1)}, f32[4,16,1,512]{3,2,1,0:T(1,128)S(1)}, u32[]{:S(2)}, u32[]{:S(2)}) collective-permute-start(f32[4,16,1,512]{3,2,1,0:T(1,128)S(1)} %get-tuple-element.26), channel_id=1, source_target_pairs={{1,0},{2,1},{3,2},{4,3},{5,4},{6,5},{7,6},{8,7},{9,8},{10,9},{11,1... | collective-permute-start | bytes 393224 | tf_op jit(solution)/shard_map/ppermute | solution.py:28
  76.5 1.9 %collective-permute-start.10 = (f32[4,1,8,512]{3,2,1,0:T(8,128)S(1)}, f32[4,1,8,512]{3,2,1,0:T(8,128)S(1)}, u32[]{:S(2)}, u32[]{:S(2)}) collective-permute-start(f32[4,1,8,512]{3,2,1,0:T(8,128)S(1)} %get-tuple-element.29), channel_id=1, source_target_pairs={{32,0},{64,32},{96,64},{128,96},{160,128},{192,160},{224,192},{256... | collective-permute-start | bytes 196616 | tf_op jit(solution)/shard_map/ppermute | solution.py:28
  78.4 12.4 %collective-permute-start.9 = (f32[4,1,8,512]{3,2,1,0:T(8,128)S(1)}, f32[4,1,8,512]{3,2,1,0:T(8,128)S(1)}, u32[]{:S(2)}, u32[]{:S(2)}) collective-permute-start(f32[4,1,8,512]{3,2,1,0:T(8,128)S(1)} %get-tuple-element.28), channel_id=1, source_target_pairs={{0,32},{32,64},{64,96},{96,128},{128,160},{160,192},{192,224},{224... | collective-permute-start | bytes 196616 | tf_op jit(solution)/shard_map/ppermute | solution.py:27
  91.4 0.7 collective-permute-done.9
  93.3 0.8 copy-done.1
  94.3 0.9 fusion.22
  95.2 0.6 fusion.127
  96.1 1.9 %collective-permute-start.12 = (f32[4,16,1,512]{3,2,1,0:T(1,128)S(1)}, f32[4,16,1,512]{3,2,1,0:T(1,128)S(1)}, u32[]{:S(2)}, u32[]{:S(2)}) collective-permute-start(f32[4,16,1,512]{3,2,1,0:T(1,128)S(1)} %get-tuple-element.23), channel_id=1, source_target_pairs={{0,1},{1,2},{2,3},{3,4},{4,5},{5,6},{6,7},{7,8},{8,9},{9,10},{10,1... | collective-permute-start | bytes 393224 | tf_op jit(solution)/shard_map/ppermute | solution.py:27
  98.0 5.5 %collective-permute-start.15 = (f32[4,16,1,512]{3,2,1,0:T(1,128)S(1)}, f32[4,16,1,512]{3,2,1,0:T(1,128)S(1)}, u32[]{:S(2)}, u32[]{:S(2)}) collective-permute-start(f32[4,16,1,512]{3,2,1,0:T(1,128)S(1)} %get-tuple-element.22), channel_id=1, source_target_pairs={{1,0},{2,1},{3,2},{4,3},{5,4},{6,5},{7,6},{8,7},{9,8},{10,9},{11,1... | collective-permute-start | bytes 393224 | tf_op jit(solution)/shard_map/ppermute | solution.py:28
  103.5 13.5 %collective-permute-start.13 = (f32[4,1,8,512]{3,2,1,0:T(8,128)S(1)}, f32[4,1,8,512]{3,2,1,0:T(8,128)S(1)}, u32[]{:S(2)}, u32[]{:S(2)}) collective-permute-start(f32[4,1,8,512]{3,2,1,0:T(8,128)S(1)} %get-tuple-element.24), channel_id=1, source_target_pairs={{0,32},{32,64},{64,96},{96,128},{128,160},{160,192},{192,224},{224... | collective-permute-start | bytes 196616 | tf_op jit(solution)/shard_map/ppermute | solution.py:27
  117.0 2.1 %collective-permute-start.14 = (f32[4,1,8,512]{3,2,1,0:T(8,128)S(1)}, f32[4,1,8,512]{3,2,1,0:T(8,128)S(1)}, u32[]{:S(2)}, u32[]{:S(2)}) collective-permute-start(f32[4,1,8,512]{3,2,1,0:T(8,128)S(1)} %get-tuple-element.25), channel_id=1, source_target_pairs={{32,0},{64,32},{96,64},{128,96},{160,128},{192,160},{224,192},{256... | collective-permute-start | bytes 196616 | tf_op jit(solution)/shard_map/ppermute | solution.py:28
  119.5 13.9 %collective-permute-done.14 = f32[4,1,8,512]{3,2,1,0:T(8,128)S(1)} collective-permute-done((f32[4,1,8,512]{3,2,1,0:T(8,128)S(1)}, f32[4,1,8,512]{3,2,1,0:T(8,128)S(1)}, u32[]{:S(2)}, u32[]{:S(2)}) %collective-permute-start.14) | collective-permute-done | bytes 65568 | tf_op jit(solution)/shard_map/ppermute | solution.py:28
  133.6 0.3 multiply_multiply_fusion
  134.6 0.9 fusion.31
  135.5 0.6 fusion.6
  136.1 0.7 slice_bitcast_fusion
  137.2 1.1 multiply_subtract_fusion
  (84 shorter events, 7.7 us)
Async XLA Ops:
  0.6 1.3 copy-start.5
  2.0 37.3 %collective-permute-start.2 = (f32[2,16,1,512]{3,2,1,0:T(1,128)S(1)}, f32[2,16,1,512]{3,2,1,0:T(1,128)S(1)}, u32[]{:S(2)}, u32[]{:S(2)}) collective-permute-start(f32[2,16,1,512]{3,2,1,0:T(1,128)S(1)} %get-tuple-element.39), channel_id=1, source_target_pairs={{0,1},{1,2},{2,3},{3,4},{4,5},{5,6},{6,7},{7,8},{8,9},{9,10},{10,1... | collective-permute-start | bytes 196616 | tf_op jit(solution)/shard_map/ppermute | solution.py:27
  5.2 34.1 %collective-permute-start.3 = (f32[2,16,1,512]{3,2,1,0:T(1,128)S(1)}, f32[2,16,1,512]{3,2,1,0:T(1,128)S(1)}, u32[]{:S(2)}, u32[]{:S(2)}) collective-permute-start(f32[2,16,1,512]{3,2,1,0:T(1,128)S(1)} %get-tuple-element.40), channel_id=1, source_target_pairs={{1,0},{2,1},{3,2},{4,3},{5,4},{6,5},{7,6},{8,7},{9,8},{10,9},{11,1... | collective-permute-start | bytes 196616 | tf_op jit(solution)/shard_map/ppermute | solution.py:28
  9.4 18.4 %collective-permute-start = (f32[2,1,8,512]{3,2,1,0:T(8,128)S(1)}, f32[2,1,8,512]{3,2,1,0:T(8,128)S(1)}, u32[]{:S(2)}, u32[]{:S(2)}) collective-permute-start(f32[2,1,8,512]{3,2,1,0:T(8,128)S(1)} %get-tuple-element.42), channel_id=1, source_target_pairs={{0,32},{32,64},{64,96},{96,128},{128,160},{160,192},{192,224},{224... | collective-permute-start | bytes 98312 | tf_op jit(solution)/shard_map/ppermute | solution.py:27
  25.1 13.9 %collective-permute-start.1 = (f32[2,1,8,512]{3,2,1,0:T(8,128)S(1)}, f32[2,1,8,512]{3,2,1,0:T(8,128)S(1)}, u32[]{:S(2)}, u32[]{:S(2)}) collective-permute-start(f32[2,1,8,512]{3,2,1,0:T(8,128)S(1)} %get-tuple-element.41), channel_id=1, source_target_pairs={{32,0},{64,32},{96,64},{128,96},{160,128},{192,160},{224,192},{256... | collective-permute-start | bytes 98312 | tf_op jit(solution)/shard_map/ppermute | solution.py:28
  39.7 1.1 copy-start.4
  39.7 1.2 copy-start.6
  41.1 24.4 %copy-start.2 = (f32[4,16,8,512]{3,2,1,0:T(8,128)}, f32[4,16,8,512]{3,2,1,0:T(8,128)S(1)}, u32[]{:S(2)}) copy-start(f32[4,16,8,512]{3,2,1,0:T(8,128)S(1)} %fusion.75) | copy-start | bytes 3145732
  41.3 12.0 %collective-permute-start.4 = (f32[4,16,1,512]{3,2,1,0:T(1,128)S(1)}, f32[4,16,1,512]{3,2,1,0:T(1,128)S(1)}, u32[]{:S(2)}, u32[]{:S(2)}) collective-permute-start(f32[4,16,1,512]{3,2,1,0:T(1,128)S(1)} %get-tuple-element.31), channel_id=1, source_target_pairs={{0,1},{1,2},{2,3},{3,4},{4,5},{5,6},{6,7},{7,8},{8,9},{9,10},{10,1... | collective-permute-start | bytes 393224 | tf_op jit(solution)/shard_map/ppermute | solution.py:27
  43.2 10.2 %collective-permute-start.7 = (f32[4,16,1,512]{3,2,1,0:T(1,128)S(1)}, f32[4,16,1,512]{3,2,1,0:T(1,128)S(1)}, u32[]{:S(2)}, u32[]{:S(2)}) collective-permute-start(f32[4,16,1,512]{3,2,1,0:T(1,128)S(1)} %get-tuple-element.30), channel_id=1, source_target_pairs={{1,0},{2,1},{3,2},{4,3},{5,4},{6,5},{7,6},{8,7},{9,8},{10,9},{11,1... | collective-permute-start | bytes 393224 | tf_op jit(solution)/shard_map/ppermute | solution.py:28
  48.7 4.8 %collective-permute-start.5 = (f32[4,1,8,512]{3,2,1,0:T(8,128)S(1)}, f32[4,1,8,512]{3,2,1,0:T(8,128)S(1)}, u32[]{:S(2)}, u32[]{:S(2)}) collective-permute-start(f32[4,1,8,512]{3,2,1,0:T(8,128)S(1)} %get-tuple-element.32), channel_id=1, source_target_pairs={{0,32},{32,64},{64,96},{96,128},{128,160},{160,192},{192,224},{224... | collective-permute-start | bytes 196616 | tf_op jit(solution)/shard_map/ppermute | solution.py:27
  51.2 14.3 %collective-permute-start.6 = (f32[4,1,8,512]{3,2,1,0:T(8,128)S(1)}, f32[4,1,8,512]{3,2,1,0:T(8,128)S(1)}, u32[]{:S(2)}, u32[]{:S(2)}) collective-permute-start(f32[4,1,8,512]{3,2,1,0:T(8,128)S(1)} %get-tuple-element.33), channel_id=1, source_target_pairs={{32,0},{64,32},{96,64},{128,96},{160,128},{192,160},{224,192},{256... | collective-permute-start | bytes 196616 | tf_op jit(solution)/shard_map/ppermute | solution.py:28
  66.2 1.2 copy-start.3
  66.2 1.5 %slice-start.1 = ((f32[4,16,8,512]{3,2,1,0:T(8,128)}), f32[3,16,8,512]{3,2,1,0:T(8,128)S(1)}, s32[]{:S(2)}) async-start(f32[4,16,8,512]{3,2,1,0:T(8,128)} %copy-done.2), calls=%async_computation.1 | async-start | bytes 1572864 | tf_op jit(solution)/shard_map/slice | solution.py:50
  68.9 23.2 %copy-start = (f32[4,16,8,512]{3,2,1,0:T(8,128)}, f32[4,16,8,512]{3,2,1,0:T(8,128)S(1)}, u32[]{:S(2)}) copy-start(f32[4,16,8,512]{3,2,1,0:T(8,128)S(1)} %fusion.74) | copy-start | bytes 3145732
  69.1 22.1 %collective-permute-start.8 = (f32[4,16,1,512]{3,2,1,0:T(1,128)S(1)}, f32[4,16,1,512]{3,2,1,0:T(1,128)S(1)}, u32[]{:S(2)}, u32[]{:S(2)}) collective-permute-start(f32[4,16,1,512]{3,2,1,0:T(1,128)S(1)} %get-tuple-element.27), channel_id=1, source_target_pairs={{0,1},{1,2},{2,3},{3,4},{4,5},{5,6},{6,7},{7,8},{8,9},{9,10},{10,1... | collective-permute-start | bytes 393224 | tf_op jit(solution)/shard_map/ppermute | solution.py:27
  71.0 20.2 %collective-permute-start.11 = (f32[4,16,1,512]{3,2,1,0:T(1,128)S(1)}, f32[4,16,1,512]{3,2,1,0:T(1,128)S(1)}, u32[]{:S(2)}, u32[]{:S(2)}) collective-permute-start(f32[4,16,1,512]{3,2,1,0:T(1,128)S(1)} %get-tuple-element.26), channel_id=1, source_target_pairs={{1,0},{2,1},{3,2},{4,3},{5,4},{6,5},{7,6},{8,7},{9,8},{10,9},{11,1... | collective-permute-start | bytes 393224 | tf_op jit(solution)/shard_map/ppermute | solution.py:28
  76.5 14.9 %collective-permute-start.10 = (f32[4,1,8,512]{3,2,1,0:T(8,128)S(1)}, f32[4,1,8,512]{3,2,1,0:T(8,128)S(1)}, u32[]{:S(2)}, u32[]{:S(2)}) collective-permute-start(f32[4,1,8,512]{3,2,1,0:T(8,128)S(1)} %get-tuple-element.29), channel_id=1, source_target_pairs={{32,0},{64,32},{96,64},{128,96},{160,128},{192,160},{224,192},{256... | collective-permute-start | bytes 196616 | tf_op jit(solution)/shard_map/ppermute | solution.py:28
  78.4 13.7 %collective-permute-start.9 = (f32[4,1,8,512]{3,2,1,0:T(8,128)S(1)}, f32[4,1,8,512]{3,2,1,0:T(8,128)S(1)}, u32[]{:S(2)}, u32[]{:S(2)}) collective-permute-start(f32[4,1,8,512]{3,2,1,0:T(8,128)S(1)} %get-tuple-element.28), channel_id=1, source_target_pairs={{0,32},{32,64},{64,96},{96,128},{128,160},{160,192},{192,224},{224... | collective-permute-start | bytes 196616 | tf_op jit(solution)/shard_map/ppermute | solution.py:27
  92.9 1.2 copy-start.1
  92.9 1.5 %slice-start = ((f32[4,16,8,512]{3,2,1,0:T(8,128)}), f32[3,16,8,512]{3,2,1,0:T(8,128)S(1)}, s32[]{:S(2)}) async-start(f32[4,16,8,512]{3,2,1,0:T(8,128)} %copy-done), calls=%async_computation | async-start | bytes 1572864 | tf_op jit(solution)/shard_map/slice | solution.py:50
  96.1 23.2 %collective-permute-start.12 = (f32[4,16,1,512]{3,2,1,0:T(1,128)S(1)}, f32[4,16,1,512]{3,2,1,0:T(1,128)S(1)}, u32[]{:S(2)}, u32[]{:S(2)}) collective-permute-start(f32[4,16,1,512]{3,2,1,0:T(1,128)S(1)} %get-tuple-element.23), channel_id=1, source_target_pairs={{0,1},{1,2},{2,3},{3,4},{4,5},{5,6},{6,7},{7,8},{8,9},{9,10},{10,1... | collective-permute-start | bytes 393224 | tf_op jit(solution)/shard_map/ppermute | solution.py:27
  98.0 21.4 %collective-permute-start.15 = (f32[4,16,1,512]{3,2,1,0:T(1,128)S(1)}, f32[4,16,1,512]{3,2,1,0:T(1,128)S(1)}, u32[]{:S(2)}, u32[]{:S(2)}) collective-permute-start(f32[4,16,1,512]{3,2,1,0:T(1,128)S(1)} %get-tuple-element.22), channel_id=1, source_target_pairs={{1,0},{2,1},{3,2},{4,3},{5,4},{6,5},{7,6},{8,7},{9,8},{10,9},{11,1... | collective-permute-start | bytes 393224 | tf_op jit(solution)/shard_map/ppermute | solution.py:28
  103.5 16.0 %collective-permute-start.13 = (f32[4,1,8,512]{3,2,1,0:T(8,128)S(1)}, f32[4,1,8,512]{3,2,1,0:T(8,128)S(1)}, u32[]{:S(2)}, u32[]{:S(2)}) collective-permute-start(f32[4,1,8,512]{3,2,1,0:T(8,128)S(1)} %get-tuple-element.24), channel_id=1, source_target_pairs={{0,32},{32,64},{64,96},{96,128},{128,160},{160,192},{192,224},{224... | collective-permute-start | bytes 196616 | tf_op jit(solution)/shard_map/ppermute | solution.py:27
  117.0 16.4 %collective-permute-start.14 = (f32[4,1,8,512]{3,2,1,0:T(8,128)S(1)}, f32[4,1,8,512]{3,2,1,0:T(8,128)S(1)}, u32[]{:S(2)}, u32[]{:S(2)}) collective-permute-start(f32[4,1,8,512]{3,2,1,0:T(8,128)S(1)} %get-tuple-element.25), channel_id=1, source_target_pairs={{32,0},{64,32},{96,64},{128,96},{160,128},{192,160},{224,192},{256... | collective-permute-start | bytes 196616 | tf_op jit(solution)/shard_map/ppermute | solution.py:28

commit v2 on v0

v2 whole, which is shorter than its diff:
```python
import functools

import jax
import jax.numpy as jnp
from jax import lax
from jax.experimental import pallas as pl
from jax.experimental.pallas import tpu as pltpu
from jax.sharding import PartitionSpec as P

SWEEPS = 3
RELAX_INNER = 8

RESIDUAL_STIFFNESS = 0.001
TOUGH_OVER_LENGTH = 0.5
TOUGH_TIMES_LENGTH = 0.25
MASS_SHIFT = 0.5
STIFF_SCALE = 0.25
CENTER_VALUE = 1.0
HALF_WIDTH = 0.75
NORMAL_WEIGHT = 1.5
RELAX_STEP = 0.5
NORMAL_FLOOR = 0.05

MESH = pl.DeviceIdType.MESH


def soft_of(d):
    return (1.0 - d) ** 2


def kernel(
    nx, ny,
    bw_ref, dmg_ref, strain_ref, sd_ref, sdisp_ref,
    out_mu_ref, out_disp_ref,
    dfr, dyl, dyh, sfr, syl, syh, faces, upd, invs, send_sem, recv_sem,
):
    X, Y, Z = dmg_ref.shape
    bx = lax.axis_index("gx")
    by = lax.axis_index("gy")
    has = (bx < nx - 1, bx > 0, by < ny - 1, by > 0)
    peers = ((bx + 1, by), (bx - 1, by), (bx, by + 1), (bx, by - 1))

    @pl.when(bx == 0)
    def _():
        dfr[:, 0] = jnp.zeros((2, Y, Z), jnp.float32)
        sfr[:, :, 0] = jnp.zeros((SWEEPS, 4, Y, Z), jnp.float32)

    @pl.when(bx == nx - 1)
    def _():
        dfr[:, X + 1] = jnp.zeros((2, Y, Z), jnp.float32)
        sfr[:, :, X + 1] = jnp.zeros((SWEEPS, 4, Y, Z), jnp.float32)

    @pl.when(by == 0)
    def _():
        dyl[...] = jnp.zeros(dyl.shape, jnp.float32)
        syl[...] = jnp.zeros(syl.shape, jnp.float32)

    @pl.when(by == ny - 1)
    def _():
        dyh[...] = jnp.zeros(dyh.shape, jnp.float32)
        syh[...] = jnp.zeros(syh.shape, jnp.float32)

    barrier = pltpu.get_barrier_semaphore()
    count = jnp.int32(0)
    for d in range(4):
        @pl.when(has[d])
        def _():
            pl.semaphore_signal(barrier, inc=1, device_id=peers[d], device_id_type=MESH)
        count = count + has[d].astype(jnp.int32)
    pl.semaphore_wait(barrier, count)

    def exchange(slot, routes):
        copies = []
        for d in range(4):
            src, dst = routes[d]
            copies.append(
                pltpu.make_async_remote_copy(
                    src_ref=src, dst_ref=dst,
                    send_sem=send_sem.at[slot, d], recv_sem=recv_sem.at[slot, d],
                    device_id=peers[d], device_id_type=MESH,
                )
            )
        for d in range(4):
            @pl.when(has[d])
            def _():
                copies[d].start()
        return copies

    def finish(copies):
        opposite = (1, 0, 3, 2)
        for d in range(4):
            @pl.when(has[d])
            def _():
                copies[d].wait_send()

            @pl.when(has[opposite[d]])
            def _():
                copies[d].wait_recv()

    c_dmg = exchange(0, (
        (dmg_ref.at[X - 1:X], dfr.at[0, 0:1]),
        (dmg_ref.at[0:1], dfr.at[0, X + 1:X + 2]),
        (dmg_ref.at[:, Y - 1:Y], dyl.at[0]),
        (dmg_ref.at[:, 0:1], dyh.at[0]),
    ))
    c_str = exchange(1, (
        (strain_ref.at[0, X - 1:X], dfr.at[1, 0:1]),
        (strain_ref.at[0, 0:1], dfr.at[1, X + 1:X + 2]),
        (strain_ref.at[1, :, Y - 1:Y], dyl.at[1]),
        (strain_ref.at[1, :, 0:1], dyh.at[1]),
    ))
    dfr[0, 1:X + 1] = dmg_ref[...]
    dfr[1, 1:X + 1] = strain_ref[0]
    finish(c_dmg)
    finish(c_str)

    rows = lax.broadcasted_iota(jnp.int32, (Y, Z), 0)
    lanes = lax.broadcasted_iota(jnp.int32, (Y, Z), 1)

    def sides(center, nxp, nxm, lo, hi):
        yp = jnp.where(rows == Y - 1, hi, pltpu.roll(center, Y - 1, 0))
        ym = jnp.where(rows == 0, lo, pltpu.roll(center, 1, 0))
        zp = jnp.where(lanes == Z - 1, 0.0, pltpu.roll(center, Z - 1, 1))
        zm = jnp.where(lanes == 0, 0.0, pltpu.roll(center, 1, 1))
        return [nxp, nxm, yp, ym, zp, zm]

    def damage_sides(i):
        d = dfr[0, i + 1]
        return d, sides(d, dfr[0, i + 2], dfr[0, i], dyl[0, i], dyh[0, i])

    def prep(i, carry):
        d, ds = damage_sides(i)
        soft_center = soft_of(d) + RESIDUAL_STIFFNESS
        fs = [0.5 * (soft_center + soft_of(s) + RESIDUAL_STIFFNESS) for s in ds]
        total = fs[0]
        for k in range(6):
            faces[k, i] = fs[k]
            if k:
                total = total + fs[k]
        sx = strain_ref[0, i]
        sy = strain_ref[1, i]
        sz = strain_ref[2, i]
        energy = 0.5 * (sx * sx + sy * sy + sz * sz)
        inv_mu = 1.0 / (TOUGH_OVER_LENGTH + 2.0 * energy + 6.0 * TOUGH_TIMES_LENGTH)
        inv_lam = 1.0 / (MASS_SHIFT + STIFF_SCALE * total)
        invs[0, i] = inv_mu
        invs[1, i] = inv_lam
        invs[2, i] = TOUGH_OVER_LENGTH + 2.0 * energy
        mu0 = inv_mu * sd_ref[i] / CENTER_VALUE
        upd[0, i] = mu0
        sfr[0, 0, i + 1] = mu0
        for c in range(3):
            lam0 = inv_lam * sdisp_ref[c, i] / CENTER_VALUE
            upd[1 + c, i] = lam0
            sfr[0, 1 + c, i + 1] = lam0
        return carry

    lax.fori_loop(0, X, prep, 0)

    def state_routes(r):
        return (
            (sfr.at[r, :, X:X + 1], sfr.at[r, :, 0:1]),
            (sfr.at[r, :, 1:2], sfr.at[r, :, X + 1:X + 2]),
            (sfr.at[r, :, 1:X + 1, Y - 1:Y], syl.at[r]),
            (sfr.at[r, :, 1:X + 1, 0:1], syh.at[r]),
        )

    ratio = CENTER_VALUE / HALF_WIDTH
    rho = 1.0 / ratio
    for sweep in range(SWEEPS):
        r = sweep
        copies = exchange(2 + r, state_routes(r))
        finish(copies)
        rho_next = 1.0 / (2.0 * ratio - rho)
        keep = rho_next * rho
        gain = 2.0 * rho_next / HALF_WIDTH
        rho = rho_next
        last = sweep == SWEEPS - 1

        def step(i, carry, r=r, keep=keep, gain=gain, last=last):
            mu = sfr[r, 0, i + 1]
            mus = sides(mu, sfr[r, 0, i + 2], sfr[r, 0, i], syl[r, 0, i], syh[r, 0, i])
            energy_diag = invs[2, i]
            damage_part = energy_diag * mu + TOUGH_TIMES_LENGTH * sum(mu - s for s in mus)
            fs = [faces[k, i] for k in range(6)]
            wxm = 2.0 * (dfr[0, i] - 1.0) * dfr[1, i] * mus[1]
            wxp = 2.0 * (dfr[0, i + 2] - 1.0) * dfr[1, i + 2] * mus[0]
            d = dfr[0, i + 1]
            wy = 2.0 * (d - 1.0) * strain_ref[1, i] * mu
            wy_lo = 2.0 * (dyl[0, i] - 1.0) * dyl[1, i] * syl[r, 0, i]
            wy_hi = 2.0 * (dyh[0, i] - 1.0) * dyh[1, i] * syh[r, 0, i]
            wy_p = jnp.where(rows == Y - 1, wy_hi, pltpu.roll(wy, Y - 1, 0))
            wy_m = jnp.where(rows == 0, wy_lo, pltpu.roll(wy, 1, 0))
            wz = 2.0 * (d - 1.0) * strain_ref[2, i] * mu
            wz_p = jnp.where(lanes == Z - 1, 0.0, pltpu.roll(wz, Z - 1, 1))
            wz_m = jnp.where(lanes == 0, 0.0, pltpu.roll(wz, 1, 1))
            transfer = (
                0.5 * (wxm - wxp),
                0.5 * (wy_m - wy_p),
                0.5 * (wz_m - wz_p),
            )
            inv_mu = invs[0, i]
            inv_lam = invs[1, i]
            residual_mu = sd_ref[i] - damage_part
            new_upd = keep * upd[0, i] + gain * inv_mu * residual_mu
            new_mu = mu + new_upd
            upd[0, i] = new_upd
            lams = []
            for c in range(3):
                lam = sfr[r, 1 + c, i + 1]
                ls = sides(lam, sfr[r, 1 + c, i + 2], sfr[r, 1 + c, i],
                           syl[r, 1 + c, i], syh[r, 1 + c, i])
                disp = MASS_SHIFT * lam + STIFF_SCALE * sum(
                    fs[k] * (lam - ls[k]) for k in range(6))
                residual = sdisp_ref[c, i] - (disp + transfer[c])
                nu = keep * upd[1 + c, i] + gain * inv_lam * residual
                upd[1 + c, i] = nu
                lams.append(lam + nu)
            if not last:
                sfr[r + 1, 0, i + 1] = new_mu
                for c in range(3):
                    sfr[r + 1, 1 + c, i + 1] = lams[c]
            else:
                out_mu_ref[i] = new_mu
                _, ds = damage_sides(i)
                grad = [0.5 * (ds[0] - ds[1]), 0.5 * (ds[2] - ds[3]), 0.5 * (ds[4] - ds[5])]
                length = jnp.sqrt(jnp.maximum(
                    grad[0] * grad[0] + grad[1] * grad[1] + grad[2] * grad[2], NORMAL_FLOOR))
                normal = [g / length for g in grad]
                size = normal[0] * normal[0] + normal[1] * normal[1] + normal[2] * normal[2]
                along = normal[0] * lams[0] + normal[1] * lams[1] + normal[2] * lams[2]
                a = RELAX_STEP / RELAX_INNER
                factor = 1.0 - a * (1.0 + NORMAL_WEIGHT * size)
                power = factor
                for _ in range(3):
                    power = power * power
                total = power
                work = bw_ref[0, 0]
                for level in range(2, 5):
                    total = jnp.where(work >= level, total * power, total)
                pull = NORMAL_WEIGHT * (1.0 - total) / (1.0 + NORMAL_WEIGHT * size)
                for c in range(3):
                    out_disp_ref[c, i] = lams[c] - (pull * along) * normal[c]
            return carry

        lax.fori_loop(0, X, step, 0)


def body(damage, strain, seed_damage, seed_disp, brick_work, nx, ny):
    X, Y, Z = damage.shape
    f32 = jnp.float32
    vmem = pl.BlockSpec(memory_space=pltpu.VMEM)
    return pl.pallas_call(
        functools.partial(kernel, nx, ny),
        out_shape=(
            jax.ShapeDtypeStruct((X, Y, Z), f32),
            jax.ShapeDtypeStruct((3, X, Y, Z), f32),
        ),
        in_specs=[pl.BlockSpec(memory_space=pltpu.SMEM), vmem, vmem, vmem, vmem],
        out_specs=(vmem, vmem),
        scratch_shapes=[
            pltpu.VMEM((2, X + 2, Y, Z), f32),
            pltpu.VMEM((2, X, 1, Z), f32),
            pltpu.VMEM((2, X, 1, Z), f32),
            pltpu.VMEM((SWEEPS, 4, X + 2, Y, Z), f32),
            pltpu.VMEM((SWEEPS, 4, X, 1, Z), f32),
            pltpu.VMEM((SWEEPS, 4, X, 1, Z), f32),
            pltpu.VMEM((6, X, Y, Z), f32),
            pltpu.VMEM((4, X, Y, Z), f32),
            pltpu.VMEM((3, X, Y, Z), f32),
            pltpu.SemaphoreType.DMA((2 + SWEEPS, 4)),
            pltpu.SemaphoreType.DMA((2 + SWEEPS, 4)),
        ],
        compiler_params=pltpu.CompilerParams(
            collective_id=0, has_side_effects=True, vmem_limit_bytes=60 * 1024 * 1024
        ),
    )(brick_work, damage, strain, seed_damage, seed_disp)


def solution(mesh):
    nx = mesh.shape["gx"]
    ny = mesh.shape["gy"]
    placed = (
        P("gx", "gy", None),
        P(None, "gx", "gy", None),
        P("gx", "gy", None),
        P(None, "gx", "gy", None),
        P("gx", "gy"),
    )
    return jax.shard_map(
        functools.partial(body, nx=nx, ny=ny),
        mesh=mesh,
        in_specs=placed,
        out_specs=(P("gx", "gy", None), P(None, "gx", "gy", None)),
        check_vma=False,
    )
```

time: 180 us -> 72.1 us (0.40)
  the two profiles are of different devices: /device:TPU:29 before, /device:TPU:27 now
where the time goes in v2:
time: 72.1 us; the launch traced here: 71.9 us
  Pallas kernels  66.9 us (93%)
  local copies, waits for them, and re-layouts  3.73 us (5%)
  between operations  1.29 us (2%)
    pallas_call x1, Pallas kernels, body(): pl.pallas_call(functools.partial(kernel, nx, ny), out_shape=(jax.ShapeDty...  66.9 us
    unnamed x2, local copies, waits for them, and re-layouts  3.73 us

profile of v2, /device:TPU:27, one launch (start us, length us, event | category | flops | bytes accessed | tf_op | source)
XLA Modules:
  0.0 71.9 jit_solution(8824567671141220710)
XLA Ops:
  1.3 66.9 %shard_map.68 = (f32[16,8,512]{2,1,0:T(8,128)}, f32[3,16,8,512]{3,2,1,0:T(8,128)}) custom-call(s32[1,1]{1,0:T(1,128)S(6)} %copy.9.bw_ref, f32[16,8,512]{2,1,0:T(8,128)} %dmg_ref.1, f32[3,16,8,512]{3,2,1,0:T(8,128)} %strain_ref.1, f32[16,8,512]{2,1,0:T(8,128)} %sd_ref.1, f32[3,16,8,512]{3,2,1,0:T(8,128)} %sdisp_ref.1), custom_call_target="tpu_custom_call" | custom-call | tf_op jit(solution)/shard_map/pallas_call | solution.py:253
  68.2 1.7 %copy.10 = f32[16,8,512]{2,1,0:T(8,128)} copy(f32[16,8,512]{2,1,0:T(8,128)} %get-tuple-element.4) | data formatting | bytes 524288
  69.8 2.1 %copy.11 = f32[3,16,8,512]{3,2,1,0:T(8,128)} copy(f32[3,16,8,512]{3,2,1,0:T(8,128)} %get-tuple-element.5) | data formatting | bytes 1572864

commit v3 on v2

--- a/solution.py
+++ b/solution.py
@@ -86,16 +86,18 @@
                 copies[d].start()
         return copies
 
-    def finish(copies):
+    def arrive(copies, dirs):
         opposite = (1, 0, 3, 2)
+        for d in dirs:
+            @pl.when(has[opposite[d]])
+            def _():
+                copies[d].wait_recv()
+
+    def sent(copies):
         for d in range(4):
             @pl.when(has[d])
             def _():
                 copies[d].wait_send()
-
-            @pl.when(has[opposite[d]])
-            def _():
-                copies[d].wait_recv()
 
     c_dmg = exchange(0, (
         (dmg_ref.at[X - 1:X], dfr.at[0, 0:1]),
@@ -111,8 +113,9 @@
     ))
     dfr[0, 1:X + 1] = dmg_ref[...]
     dfr[1, 1:X + 1] = strain_ref[0]
-    finish(c_dmg)
-    finish(c_str)
+    arrive(c_dmg, (2, 3))
+    arrive(c_str, (2, 3))
+    pending = [c_dmg, c_str]
 
     rows = lax.broadcasted_iota(jnp.int32, (Y, Z), 0)
     lanes = lax.broadcasted_iota(jnp.int32, (Y, Z), 1)
@@ -155,7 +158,11 @@
             sfr[0, 1 + c, i + 1] = lam0
         return carry
 
-    lax.fori_loop(0, X, prep, 0)
+    lax.fori_loop(1, X - 1, prep, 0)
+    arrive(c_dmg, (0, 1))
+    arrive(c_str, (0, 1))
+    for i in (0, X - 1):
+        prep(i, 0)
 
     def state_routes(r):
         return (
@@ -170,7 +177,8 @@
     for sweep in range(SWEEPS):
         r = sweep
         copies = exchange(2 + r, state_routes(r))
-        finish(copies)
+        pending.append(copies)
+        arrive(copies, (2, 3))
         rho_next = 1.0 / (2.0 * ratio - rho)
         keep = rho_next * rho
         gain = 2.0 * rho_next / HALF_WIDTH
@@ -243,7 +251,13 @@
                     out_disp_ref[c, i] = lams[c] - (pull * along) * normal[c]
             return carry
 
-        lax.fori_loop(0, X, step, 0)
+        lax.fori_loop(1, X - 1, step, 0)
+        arrive(copies, (0, 1))
+        for i in (0, X - 1):
+            step(i, 0)
+
+    for copies in pending:
+        sent(copies)
 
 
 def body(damage, strain, seed_damage, seed_disp, brick_work, nx, ny):

time: 72.1 us -> 68.5 us (0.950)
  the two profiles are of different devices: /device:TPU:27 before, /device:TPU:26 now
where the time goes in v3:
time: 68.5 us; the launch traced here: 68.2 us
  Pallas kernels  63.1 us (92%)
  local copies, waits for them, and re-layouts  3.73 us (5%)
  between operations  1.29 us (2%)
    pallas_call x1, Pallas kernels, body(): pl.pallas_call(functools.partial(kernel, nx, ny), out_shape=(jax.ShapeDty...  63.1 us
    unnamed x2, local copies, waits for them, and re-layouts  3.73 us

profile of v3, /device:TPU:26, one launch (start us, length us, event | category | flops | bytes accessed | tf_op | source)
XLA Modules:
  0.0 68.2 jit_solution(9175035002006145848)
XLA Ops:
  1.3 63.1 %shard_map.68 = (f32[16,8,512]{2,1,0:T(8,128)}, f32[3,16,8,512]{3,2,1,0:T(8,128)}) custom-call(s32[1,1]{1,0:T(1,128)S(6)} %copy.9.bw_ref, f32[16,8,512]{2,1,0:T(8,128)} %dmg_ref.1, f32[3,16,8,512]{3,2,1,0:T(8,128)} %strain_ref.1, f32[16,8,512]{2,1,0:T(8,128)} %sd_ref.1, f32[3,16,8,512]{3,2,1,0:T(8,128)} %sdisp_ref.1), custom_call_target="tpu_custom_call" | custom-call | tf_op jit(solution)/shard_map/pallas_call | solution.py:267
  64.4 1.7 %copy.10 = f32[16,8,512]{2,1,0:T(8,128)} copy(f32[16,8,512]{2,1,0:T(8,128)} %get-tuple-element.4) | data formatting | bytes 524288
  66.1 2.1 %copy.11 = f32[3,16,8,512]{3,2,1,0:T(8,128)} copy(f32[3,16,8,512]{3,2,1,0:T(8,128)} %get-tuple-element.5) | data formatting | bytes 1572864

commit v4 on v2

v4 whole, which is shorter than its diff:
```python
import functools

import jax
import jax.numpy as jnp
from jax import lax
from jax.experimental import pallas as pl
from jax.experimental.pallas import tpu as pltpu
from jax.sharding import PartitionSpec as P

SWEEPS = 3
RELAX_INNER = 8

RESIDUAL_STIFFNESS = 0.001
TOUGH_OVER_LENGTH = 0.5
TOUGH_TIMES_LENGTH = 0.25
MASS_SHIFT = 0.5
STIFF_SCALE = 0.25
CENTER_VALUE = 1.0
HALF_WIDTH = 0.75
NORMAL_WEIGHT = 1.5
RELAX_STEP = 0.5
NORMAL_FLOOR = 0.05

MESH = pl.DeviceIdType.MESH

S_DMG, S_STR, S_SEED, S_MU, S_STATE = 0, 1, 2, 3, 4


def soft_of(d):
    return (1.0 - d) ** 2


def inverse_disp(d, sides):
    soft_center = soft_of(d) + RESIDUAL_STIFFNESS
    fs = [0.5 * (soft_center + soft_of(s) + RESIDUAL_STIFFNESS) for s in sides]
    total = fs[0]
    for k in range(1, 6):
        total = total + fs[k]
    return fs, 1.0 / (MASS_SHIFT + STIFF_SCALE * total)


def kernel(
    nx, ny,
    bw_ref, dmg_ref, strain_ref, sd_ref, sdisp_ref,
    out_mu_ref, out_disp_ref,
    dxf, ydl, ydh, strl, strh, sdxl, sdxh, sdyl, sdyh, cor,
    sfr, syl, syh, faces, upd, invs,
    send_sem, recv_sem, csend_sem, crecv_sem,
):
    X, Y, Z = dmg_ref.shape
    bx = lax.axis_index("gx")
    by = lax.axis_index("gy")
    has = (bx < nx - 1, bx > 0, by < ny - 1, by > 0)
    peers = ((bx + 1, by), (bx - 1, by), (bx, by + 1), (bx, by - 1))
    diag = ((bx + 1, by + 1), (bx + 1, by - 1), (bx - 1, by + 1), (bx - 1, by - 1))
    diag_has = (has[0] & has[2], has[0] & has[3], has[1] & has[2], has[1] & has[3])
    f32 = jnp.float32

    @pl.when(bx == 0)
    def _():
        dxf[:, 0:2] = jnp.zeros((2, 2, Y, Z), f32)
        sdxl[...] = jnp.zeros(sdxl.shape, f32)
        sfr[:, :, 0] = jnp.zeros((SWEEPS, 4, Y, Z), f32)

    @pl.when(bx == nx - 1)
    def _():
        dxf[:, X + 2:X + 4] = jnp.zeros((2, 2, Y, Z), f32)
        sdxh[...] = jnp.zeros(sdxh.shape, f32)
        sfr[:, :, X + 1] = jnp.zeros((SWEEPS, 4, Y, Z), f32)

    @pl.when(by == 0)
    def _():
        ydl[...] = jnp.zeros(ydl.shape, f32)
        strl[...] = jnp.zeros(strl.shape, f32)
        sdyl[...] = jnp.zeros(sdyl.shape, f32)
        syl[...] = jnp.zeros(syl.shape, f32)

    @pl.when(by == ny - 1)
    def _():
        ydh[...] = jnp.zeros(ydh.shape, f32)
        strh[...] = jnp.zeros(strh.shape, f32)
        sdyh[...] = jnp.zeros(sdyh.shape, f32)
        syh[...] = jnp.zeros(syh.shape, f32)

    for k in range(4):
        @pl.when(jnp.logical_not(diag_has[k]))
        def _():
            cor[k] = jnp.zeros((1, 1, Z), f32)

    barrier = pltpu.get_barrier_semaphore()
    count = jnp.int32(0)
    for peer, ok in zip(peers + diag, has + diag_has):
        @pl.when(ok)
        def _():
            pl.semaphore_signal(barrier, inc=1, device_id=peer, device_id_type=MESH)
        count = count + ok.astype(jnp.int32)

    dxf[0, 2:X + 2] = dmg_ref[...]
    dxf[1, 2:X + 2] = strain_ref[0]

    def local(i, carry):
        sx = strain_ref[0, i]
        sy = strain_ref[1, i]
        sz = strain_ref[2, i]
        energy = 0.5 * (sx * sx + sy * sy + sz * sz)
        inv_mu = 1.0 / (TOUGH_OVER_LENGTH + 2.0 * energy + 6.0 * TOUGH_TIMES_LENGTH)
        invs[0, i] = inv_mu
        invs[2, i] = TOUGH_OVER_LENGTH + 2.0 * energy
        mu0 = inv_mu * sd_ref[i] / CENTER_VALUE
        upd[0, i] = mu0
        sfr[0, 0, i + 1] = mu0
        return carry

    lax.fori_loop(0, X, local, 0)

    pl.semaphore_wait(barrier, count)

    def exchange(slot, routes, dirs):
        copies = {}
        for d in dirs:
            src, dst = routes[d]
            copies[d] = pltpu.make_async_remote_copy(
                src_ref=src, dst_ref=dst,
                send_sem=send_sem.at[slot, d], recv_sem=recv_sem.at[slot, d],
                device_id=peers[d], device_id_type=MESH,
            )
            @pl.when(has[d])
            def _():
                copies[d].start()
        return copies

    opposite = (1, 0, 3, 2)
    pending = []

    def arrive(copies):
        for d, copy in copies.items():
            @pl.when(has[opposite[d]])
            def _():
                copy.wait_recv()

    x_dirs, y_dirs = (0, 1), (2, 3)
    round0 = [
        (S_DMG, (
            (dmg_ref.at[X - 2:X], dxf.at[0, 0:2]),
            (dmg_ref.at[0:2], dxf.at[0, X + 2:X + 4]),
            (dmg_ref.at[:, Y - 2:Y], ydl),
            (dmg_ref.at[:, 0:2], ydh),
        )),
        (S_STR, (
            (strain_ref.at[0, X - 1:X], dxf.at[1, 1:2]),
            (strain_ref.at[0, 0:1], dxf.at[1, X + 2:X + 3]),
            (strain_ref.at[1, :, Y - 1:Y], strl),
            (strain_ref.at[1, :, 0:1], strh),
        )),
        (S_SEED, (
            (sdisp_ref.at[:, X - 1:X], sdxl),
            (sdisp_ref.at[:, 0:1], sdxh),
            (sdisp_ref.at[:, :, Y - 1:Y], sdyl),
            (sdisp_ref.at[:, :, 0:1], sdyh),
        )),
        (S_MU, (
            (sfr.at[0, 0:1, X:X + 1], sfr.at[0, 0:1, 0:1]),
            (sfr.at[0, 0:1, 1:2], sfr.at[0, 0:1, X + 1:X + 2]),
            (sfr.at[0, 0:1, 1:X + 1, Y - 1:Y], syl.at[0, 0:1]),
            (sfr.at[0, 0:1, 1:X + 1, 0:1], syh.at[0, 0:1]),
        )),
    ]
    x0 = [exchange(slot, routes, x_dirs) for slot, routes in round0]
    y0 = [exchange(slot, routes, y_dirs) for slot, routes in round0]
    corner_src = (
        dmg_ref.at[0:1, 0:1],
        dmg_ref.at[0:1, Y - 1:Y],
        dmg_ref.at[X - 1:X, 0:1],
        dmg_ref.at[X - 1:X, Y - 1:Y],
    )
    send_to = ((bx - 1, by - 1), (bx - 1, by + 1), (bx + 1, by - 1), (bx + 1, by + 1))
    send_has = (diag_has[3], diag_has[2], diag_has[1], diag_has[0])
    corners = []
    for k in range(4):
        copy = pltpu.make_async_remote_copy(
            src_ref=corner_src[k], dst_ref=cor.at[k],
            send_sem=csend_sem.at[k], recv_sem=crecv_sem.at[k],
            device_id=send_to[k], device_id_type=MESH,
        )
        corners.append(copy)

        @pl.when(send_has[k])
        def _():
            copy.start()
    pending += x0 + y0

    rows = lax.broadcasted_iota(jnp.int32, (Y, Z), 0)
    lanes = lax.broadcasted_iota(jnp.int32, (Y, Z), 1)
    lanes1 = lax.broadcasted_iota(jnp.int32, (1, Z), 1)

    def zsides(v, ln):
        n = v.shape[-1]
        zp = jnp.where(ln == n - 1, 0.0, pltpu.roll(v, n - 1, v.ndim - 1))
        zm = jnp.where(ln == 0, 0.0, pltpu.roll(v, 1, v.ndim - 1))
        return zp, zm

    def sides(center, nxp, nxm, lo, hi):
        yp = jnp.where(rows == Y - 1, hi, pltpu.roll(center, Y - 1, 0))
        ym = jnp.where(rows == 0, lo, pltpu.roll(center, 1, 0))
        zp, zm = zsides(center, lanes)
        return [nxp, nxm, yp, ym, zp, zm]

    def damage_sides(i):
        d = dxf[0, i + 2]
        return d, sides(d, dxf[0, i + 3], dxf[0, i + 1], ydl[i, 1:2], ydh[i, 0:1])

    for k in range(4):
        @pl.when(diag_has[k])
        def _():
            corners[k].wait_recv()
    arrive_y0 = [arrive(c) for c in y0]

    def y_row_lam(i, carry):
        for hi in (False, True):
            buf = ydh if hi else ydl
            near = 0 if hi else 1
            far = 1 if hi else 0
            d = buf[i, near:near + 1]
            right = cor[0 if hi else 1, 0]
            left = cor[2 if hi else 3, 0]
            nxp = jnp.where(i == X - 1, right, buf[(i + 1) % X, near:near + 1])
            nxm = jnp.where(i == 0, left, buf[(i + X - 1) % X, near:near + 1])
            own = dmg_ref[i, Y - 1:Y] if hi else dmg_ref[i, 0:1]
            beyond = buf[i, far:far + 1]
            yp, ym = (beyond, own) if hi else (own, beyond)
            zp, zm = zsides(d, lanes1)
            _, inv = inverse_disp(d, [nxp, nxm, yp, ym, zp, zm])
            seeds = sdyh if hi else sdyl
            target = syh if hi else syl
            for c in range(3):
                target[0, 1 + c, i] = inv * seeds[c, i] / CENTER_VALUE
        return carry

    lax.fori_loop(0, X, y_row_lam, 0)

    def prep(i, carry):
        d, ds = damage_sides(i)
        fs, inv_lam = inverse_disp(d, ds)
        for k in range(6):
            faces[k, i] = fs[k]
        invs[1, i] = inv_lam
        for c in range(3):
            lam0 = inv_lam * sdisp_ref[c, i] / CENTER_VALUE
            upd[1 + c, i] = lam0
            sfr[0, 1 + c, i + 1] = lam0
        return carry

    lax.fori_loop(1, X - 1, prep, 0)
    for c in x0:
        arrive(c)
    for i in (0, X - 1):
        prep(i, 0)

    for hi in (False, True):
        j = X + 2 if hi else 1
        d = dxf[0, j]
        nxp = dxf[0, j + 1]
        nxm = dxf[0, j - 1]
        up = cor[0 if hi else 2]
        down = cor[1 if hi else 3]
        yp = jnp.where(rows == Y - 1, up[0], pltpu.roll(d, Y - 1, 0))
        ym = jnp.where(rows == 0, down[0], pltpu.roll(d, 1, 0))
        zp, zm = zsides(d, lanes)
        _, inv = inverse_disp(d, [nxp, nxm, yp, ym, zp, zm])
        seeds = sdxh if hi else sdxl
        plane = X + 1 if hi else 0
        for c in range(3):
            sfr[0, 1 + c, plane] = inv * seeds[c, 0] / CENTER_VALUE

    def state_routes(r):
        return (
            (sfr.at[r, :, X:X + 1], sfr.at[r, :, 0:1]),
            (sfr.at[r, :, 1:2], sfr.at[r, :, X + 1:X + 2]),
            (sfr.at[r, :, 1:X + 1, Y - 1:Y], syl.at[r]),
            (sfr.at[r, :, 1:X + 1, 0:1], syh.at[r]),
        )

    ratio = CENTER_VALUE / HALF_WIDTH
    rho = 1.0 / ratio
    for sweep in range(SWEEPS):
        r = sweep
        rho_next = 1.0 / (2.0 * ratio - rho)
        keep = rho_next * rho
        gain = 2.0 * rho_next / HALF_WIDTH
        rho = rho_next
        last = sweep == SWEEPS - 1

        def step(i, carry, r=r, keep=keep, gain=gain, last=last):
            mu = sfr[r, 0, i + 1]
            mus = sides(mu, sfr[r, 0, i + 2], sfr[r, 0, i], syl[r, 0, i], syh[r, 0, i])
            damage_part = invs[2, i] * mu + TOUGH_TIMES_LENGTH * sum(mu - s for s in mus)
            fs = [faces[k, i] for k in range(6)]
            wxm = 2.0 * (dxf[0, i + 1] - 1.0) * dxf[1, i + 1] * mus[1]
            wxp = 2.0 * (dxf[0, i + 3] - 1.0) * dxf[1, i + 3] * mus[0]
            d = dxf[0, i + 2]
            wy = 2.0 * (d - 1.0) * strain_ref[1, i] * mu
            wy_lo = 2.0 * (ydl[i, 1:2] - 1.0) * strl[i] * syl[r, 0, i]
            wy_hi = 2.0 * (ydh[i, 0:1] - 1.0) * strh[i] * syh[r, 0, i]
            wy_p = jnp.where(rows == Y - 1, wy_hi, pltpu.roll(wy, Y - 1, 0))
            wy_m = jnp.where(rows == 0, wy_lo, pltpu.roll(wy, 1, 0))
            wz = 2.0 * (d - 1.0) * strain_ref[2, i] * mu
            wz_p, wz_m = zsides(wz, lanes)
            transfer = (
                0.5 * (wxm - wxp),
                0.5 * (wy_m - wy_p),
                0.5 * (wz_m - wz_p),
            )
            inv_mu = invs[0, i]
            inv_lam = invs[1, i]
            residual_mu = sd_ref[i] - damage_part
            new_upd = keep * upd[0, i] + gain * inv_mu * residual_mu
            new_mu = mu + new_upd
            upd[0, i] = new_upd
            lams = []
            for c in range(3):
                lam = sfr[r, 1 + c, i + 1]
                ls = sides(lam, sfr[r, 1 + c, i + 2], sfr[r, 1 + c, i],
                           syl[r, 1 + c, i], syh[r, 1 + c, i])
                disp = MASS_SHIFT * lam + STIFF_SCALE * sum(
                    fs[k] * (lam - ls[k]) for k in range(6))
                residual = sdisp_ref[c, i] - (disp + transfer[c])
                nu = keep * upd[1 + c, i] + gain * inv_lam * residual
                upd[1 + c, i] = nu
                lams.append(lam + nu)
            if not last:
                sfr[r + 1, 0, i + 1] = new_mu
                for c in range(3):
                    sfr[r + 1, 1 + c, i + 1] = lams[c]
            else:
                out_mu_ref[i] = new_mu
                _, ds = damage_sides(i)
                grad = [0.5 * (ds[0] - ds[1]), 0.5 * (ds[2] - ds[3]), 0.5 * (ds[4] - ds[5])]
                length = jnp.sqrt(jnp.maximum(
                    grad[0] * grad[0] + grad[1] * grad[1] + grad[2] * grad[2], NORMAL_FLOOR))
                normal = [g / length for g in grad]
                size = normal[0] * normal[0] + normal[1] * normal[1] + normal[2] * normal[2]
                along = normal[0] * lams[0] + normal[1] * lams[1] + normal[2] * lams[2]
                a = RELAX_STEP / RELAX_INNER
                factor = 1.0 - a * (1.0 + NORMAL_WEIGHT * size)
                power = factor
                for _ in range(3):
                    power = power * power
                total = power
                work = bw_ref[0, 0]
                for level in range(2, 5):
                    total = jnp.where(work >= level, total * power, total)
                pull = NORMAL_WEIGHT * (1.0 - total) / (1.0 + NORMAL_WEIGHT * size)
                for c in range(3):
                    out_disp_ref[c, i] = lams[c] - (pull * along) * normal[c]
            return carry

        if r == 0:
            for i in (0, X - 1):
                step(i, 0)
            nxt = exchange(S_STATE, state_routes(1), x_dirs)
            lax.fori_loop(1, X - 1, step, 0)
            nyt = exchange(S_STATE, state_routes(1), y_dirs)
        else:
            arrive(nyt)
            lax.fori_loop(1, X - 1, step, 0)
            arrive(nxt)
            for i in (0, X - 1):
                step(i, 0)
            pending += [nxt, nyt]
            if not last:
                nxt = exchange(S_STATE + r, state_routes(r + 1), x_dirs)
                nyt = exchange(S_STATE + r, state_routes(r + 1), y_dirs)

    for copies in pending:
        for d, copy in copies.items():
            @pl.when(has[d])
            def _():
                copy.wait_send()
    for k in range(4):
        @pl.when(send_has[k])
        def _():
            corners[k].wait_send()


def body(damage, strain, seed_damage, seed_disp, brick_work, nx, ny):
    X, Y, Z = damage.shape
    f32 = jnp.float32
    vmem = pl.BlockSpec(memory_space=pltpu.VMEM)
    return pl.pallas_call(
        functools.partial(kernel, nx, ny),
        out_shape=(
            jax.ShapeDtypeStruct((X, Y, Z), f32),
            jax.ShapeDtypeStruct((3, X, Y, Z), f32),
        ),
        in_specs=[pl.BlockSpec(memory_space=pltpu.SMEM), vmem, vmem, vmem, vmem],
        out_specs=(vmem, vmem),
        scratch_shapes=[
            pltpu.VMEM((2, X + 4, Y, Z), f32),
            pltpu.VMEM((X, 2, Z), f32),
            pltpu.VMEM((X, 2, Z), f32),
            pltpu.VMEM((X, 1, Z), f32),
            pltpu.VMEM((X, 1, Z), f32),
            pltpu.VMEM((3, 1, Y, Z), f32),
            pltpu.VMEM((3, 1, Y, Z), f32),
            pltpu.VMEM((3, X, 1, Z), f32),
            pltpu.VMEM((3, X, 1, Z), f32),
            pltpu.VMEM((4, 1, 1, Z), f32),
            pltpu.VMEM((SWEEPS, 4, X + 2, Y, Z), f32),
            pltpu.VMEM((SWEEPS, 4, X, 1, Z), f32),
            pltpu.VMEM((SWEEPS, 4, X, 1, Z), f32),
            pltpu.VMEM((6, X, Y, Z), f32),
            pltpu.VMEM((4, X, Y, Z), f32),
            pltpu.VMEM((3, X, Y, Z), f32),
            pltpu.SemaphoreType.DMA((S_STATE + SWEEPS - 1, 4)),
            pltpu.SemaphoreType.DMA((S_STATE + SWEEPS - 1, 4)),
            pltpu.SemaphoreType.DMA((4,)),
            pltpu.SemaphoreType.DMA((4,)),
        ],
        compiler_params=pltpu.CompilerParams(
            collective_id=0, has_side_effects=True, vmem_limit_bytes=60 * 1024 * 1024
        ),
    )(brick_work, damage, strain, seed_damage, seed_disp)


def solution(mesh):
    nx = mesh.shape["gx"]
    ny = mesh.shape["gy"]
    placed = (
        P("gx", "gy", None),
        P(None, "gx", "gy", None),
        P("gx", "gy", None),
        P(None, "gx", "gy", None),
        P("gx", "gy"),
    )
    return jax.shard_map(
        functools.partial(body, nx=nx, ny=ny),
        mesh=mesh,
        in_specs=placed,
        out_specs=(P("gx", "gy", None), P(None, "gx", "gy", None)),
        check_vma=False,
    )
```

time: 72.1 us -> 71.2 us (0.988)
  the two profiles are of different devices: /device:TPU:27 before, /device:TPU:28 now
where the time goes in v4:
time: 71.2 us; the launch traced here: 71 us
  Pallas kernels  65.9 us (93%)
  local copies, waits for them, and re-layouts  3.73 us (5%)
  between operations  1.29 us (2%)
    pallas_call x1, Pallas kernels, body(): pl.pallas_call(functools.partial(kernel, nx, ny), out_shape=(jax.ShapeDty...  65.9 us
    unnamed x2, local copies, waits for them, and re-layouts  3.73 us

profile of v4, /device:TPU:28, one launch (start us, length us, event | category | flops | bytes accessed | tf_op | source)
XLA Modules:
  0.0 71.0 jit_solution(7325560635678584575)
XLA Ops:
  1.3 65.9 %shard_map.68 = (f32[16,8,512]{2,1,0:T(8,128)}, f32[3,16,8,512]{3,2,1,0:T(8,128)}) custom-call(s32[1,1]{1,0:T(1,128)S(6)} %copy.9.bw_ref, f32[16,8,512]{2,1,0:T(8,128)} %dmg_ref.1, f32[3,16,8,512]{3,2,1,0:T(8,128)} %strain_ref.1, f32[16,8,512]{2,1,0:T(8,128)} %sd_ref.1, f32[3,16,8,512]{3,2,1,0:T(8,128)} %sdisp_ref.1), custom_call_target="tpu_custom_call" | custom-call | tf_op jit(solution)/shard_map/pallas_call | solution.py:389
  67.2 1.7 %copy.10 = f32[16,8,512]{2,1,0:T(8,128)} copy(f32[16,8,512]{2,1,0:T(8,128)} %get-tuple-element.4) | data formatting | bytes 524288
  68.9 2.1 %copy.11 = f32[3,16,8,512]{3,2,1,0:T(8,128)} copy(f32[3,16,8,512]{3,2,1,0:T(8,128)} %get-tuple-element.5) | data formatting | bytes 1572864

commit v5 on v4

--- a/solution.py
+++ b/solution.py
@@ -45,7 +45,7 @@
     out_mu_ref, out_disp_ref,
     dxf, ydl, ydh, strl, strh, sdxl, sdxh, sdyl, sdyh, cor,
     sfr, syl, syh, faces, upd, invs,
-    send_sem, recv_sem, csend_sem, crecv_sem,
+    send_sem, recv_sem, csend_sem, crecv_sem, edge_send, edge_recv,
 ):
     X, Y, Z = dmg_ref.shape
     bx = lax.axis_index("gx")
@@ -115,13 +115,14 @@
 
     pl.semaphore_wait(barrier, count)
 
-    def exchange(slot, routes, dirs):
+    def exchange(slot, routes, dirs, sems=None):
+        ssem, rsem = sems if sems is not None else (send_sem, recv_sem)
         copies = {}
         for d in dirs:
             src, dst = routes[d]
             copies[d] = pltpu.make_async_remote_copy(
                 src_ref=src, dst_ref=dst,
-                send_sem=send_sem.at[slot, d], recv_sem=recv_sem.at[slot, d],
+                send_sem=ssem.at[slot, d], recv_sem=rsem.at[slot, d],
                 device_id=peers[d], device_id_type=MESH,
             )
             @pl.when(has[d])
@@ -272,13 +273,25 @@
         for c in range(3):
             sfr[0, 1 + c, plane] = inv * seeds[c, 0] / CENTER_VALUE
 
-    def state_routes(r):
-        return (
-            (sfr.at[r, :, X:X + 1], sfr.at[r, :, 0:1]),
-            (sfr.at[r, :, 1:2], sfr.at[r, :, X + 1:X + 2]),
-            (sfr.at[r, :, 1:X + 1, Y - 1:Y], syl.at[r]),
-            (sfr.at[r, :, 1:X + 1, 0:1], syh.at[r]),
-        )
+    def state_routes(r, part):
+        if part == "x":
+            return (
+                (sfr.at[r, :, X:X + 1], sfr.at[r, :, 0:1]),
+                (sfr.at[r, :, 1:2], sfr.at[r, :, X + 1:X + 2]),
+            )
+        lo, hi = {"ya": (1, X - 1), "y0": (0, 1), "y1": (X - 1, X)}[part]
+        return (None, None,
+                (sfr.at[r, :, lo + 1:hi + 1, Y - 1:Y], syl.at[r, :, lo:hi]),
+                (sfr.at[r, :, lo + 1:hi + 1, 0:1], syh.at[r, :, lo:hi]))
+
+    def send_state(r, part):
+        routes = state_routes(r, part)
+        if part == "x":
+            return exchange(S_STATE + r - 1, routes + (None, None), x_dirs)
+        if part == "ya":
+            return exchange(S_STATE + r - 1, routes, y_dirs)
+        k = 0 if part == "y0" else 1
+        return exchange(r - 1, routes, y_dirs, (edge_send.at[k], edge_recv.at[k]))
 
     ratio = CENTER_VALUE / HALF_WIDTH
     rho = 1.0 / ratio
@@ -357,19 +370,22 @@
         if r == 0:
             for i in (0, X - 1):
                 step(i, 0)
-            nxt = exchange(S_STATE, state_routes(1), x_dirs)
+            edge_copies = [send_state(1, p) for p in ("x", "y0", "y1")]
             lax.fori_loop(1, X - 1, step, 0)
-            nyt = exchange(S_STATE, state_routes(1), y_dirs)
+            inner_copies = send_state(1, "ya")
         else:
-            arrive(nyt)
+            arrive(inner_copies)
             lax.fori_loop(1, X - 1, step, 0)
-            arrive(nxt)
+            pending.append(inner_copies)
+            if not last:
+                inner_copies = send_state(r + 1, "ya")
+            for c in edge_copies:
+                arrive(c)
             for i in (0, X - 1):
                 step(i, 0)
-            pending += [nxt, nyt]
+            pending += edge_copies
             if not last:
-                nxt = exchange(S_STATE + r, state_routes(r + 1), x_dirs)
-                nyt = exchange(S_STATE + r, state_routes(r + 1), y_dirs)
+                edge_copies = [send_state(r + 1, p) for p in ("x", "y0", "y1")]
 
     for copies in pending:
         for d, copy in copies.items():
@@ -415,6 +431,8 @@
             pltpu.SemaphoreType.DMA((S_STATE + SWEEPS - 1, 4)),
             pltpu.SemaphoreType.DMA((4,)),
             pltpu.SemaphoreType.DMA((4,)),
+            pltpu.SemaphoreType.DMA((2, SWEEPS - 1, 4)),
+            pltpu.SemaphoreType.DMA((2, SWEEPS - 1, 4)),
         ],
         compiler_params=pltpu.CompilerParams(
             collective_id=0, has_side_effects=True, vmem_limit_bytes=60 * 1024 * 1024

time: 71.2 us -> 72.8 us (1.022)
  the two profiles are of different devices: /device:TPU:28 before, /device:TPU:35 now
where the time goes in v5:
time: 72.8 us; the launch traced here: 72.6 us
  Pallas kernels  67.5 us (93%)
  local copies, waits for them, and re-layouts  3.73 us (5%)
  between operations  1.29 us (2%)
    pallas_call x1, Pallas kernels, body(): pl.pallas_call(functools.partial(kernel, nx, ny), out_shape=(jax.ShapeDty...  67.5 us
    unnamed x2, local copies, waits for them, and re-layouts  3.73 us

profile of v5, /device:TPU:35, one launch (start us, length us, event | category | flops | bytes accessed | tf_op | source)
XLA Modules:
  0.0 72.6 jit_solution(5400842360639248503)
XLA Ops:
  1.3 67.5 %shard_map.68 = (f32[16,8,512]{2,1,0:T(8,128)}, f32[3,16,8,512]{3,2,1,0:T(8,128)}) custom-call(s32[1,1]{1,0:T(1,128)S(6)} %copy.9.bw_ref, f32[16,8,512]{2,1,0:T(8,128)} %dmg_ref.1, f32[3,16,8,512]{3,2,1,0:T(8,128)} %strain_ref.1, f32[16,8,512]{2,1,0:T(8,128)} %sd_ref.1, f32[3,16,8,512]{3,2,1,0:T(8,128)} %sdisp_ref.1), custom_call_target="tpu_custom_call" | custom-call | tf_op jit(solution)/shard_map/pallas_call | solution.py:405
  68.8 1.7 %copy.10 = f32[16,8,512]{2,1,0:T(8,128)} copy(f32[16,8,512]{2,1,0:T(8,128)} %get-tuple-element.4) | data formatting | bytes 524288
  70.5 2.1 %copy.11 = f32[3,16,8,512]{3,2,1,0:T(8,128)} copy(f32[3,16,8,512]{3,2,1,0:T(8,128)} %get-tuple-element.5) | data formatting | bytes 1572864

commit v6 on v3

--- a/solution.py
+++ b/solution.py
@@ -31,7 +31,7 @@
 def kernel(
     nx, ny,
     bw_ref, dmg_ref, strain_ref, sd_ref, sdisp_ref,
-    out_mu_ref, out_disp_ref,
+    out_mu_ref, out_step_ref, out_disp_ref, out_corr_ref,
     dfr, dyl, dyh, sfr, syl, syh, faces, upd, invs, send_sem, recv_sem,
 ):
     X, Y, Z = dmg_ref.shape
@@ -229,7 +229,8 @@
                 for c in range(3):
                     sfr[r + 1, 1 + c, i + 1] = lams[c]
             else:
-                out_mu_ref[i] = new_mu
+                out_mu_ref[i] = mu
+                out_step_ref[i] = new_upd
                 _, ds = damage_sides(i)
                 grad = [0.5 * (ds[0] - ds[1]), 0.5 * (ds[2] - ds[3]), 0.5 * (ds[4] - ds[5])]
                 length = jnp.sqrt(jnp.maximum(
@@ -248,7 +249,8 @@
                     total = jnp.where(work >= level, total * power, total)
                 pull = NORMAL_WEIGHT * (1.0 - total) / (1.0 + NORMAL_WEIGHT * size)
                 for c in range(3):
-                    out_disp_ref[c, i] = lams[c] - (pull * along) * normal[c]
+                    out_disp_ref[c, i] = lams[c]
+                    out_corr_ref[c, i] = (pull * along) * normal[c]
             return carry
 
         lax.fori_loop(1, X - 1, step, 0)
@@ -264,14 +266,16 @@
     X, Y, Z = damage.shape
     f32 = jnp.float32
     vmem = pl.BlockSpec(memory_space=pltpu.VMEM)
-    return pl.pallas_call(
+    state = pl.pallas_call(
         functools.partial(kernel, nx, ny),
         out_shape=(
             jax.ShapeDtypeStruct((X, Y, Z), f32),
+            jax.ShapeDtypeStruct((X, Y, Z), f32),
+            jax.ShapeDtypeStruct((3, X, Y, Z), f32),
             jax.ShapeDtypeStruct((3, X, Y, Z), f32),
         ),
         in_specs=[pl.BlockSpec(memory_space=pltpu.SMEM), vmem, vmem, vmem, vmem],
-        out_specs=(vmem, vmem),
+        out_specs=(vmem, vmem, vmem, vmem),
         scratch_shapes=[
             pltpu.VMEM((2, X + 2, Y, Z), f32),
             pltpu.VMEM((2, X, 1, Z), f32),
@@ -289,6 +293,8 @@
             collective_id=0, has_side_effects=True, vmem_limit_bytes=60 * 1024 * 1024
         ),
     )(brick_work, damage, strain, seed_damage, seed_disp)
+    mu, step, lam, corr = state
+    return mu + step, lam - corr
 
 
 def solution(mesh):

time: 68.5 us -> 69 us (level)
  the two profiles are of different devices: /device:TPU:26 before, /device:TPU:99 now
where the time goes in v6:
time: 69 us; the launch traced here: 68.8 us
  Pallas kernels  63.5 us (92%)
  other arithmetic  3.99 us (6%)
  between operations  1.29 us (2%)
    pallas_call x1, Pallas kernels, body(): pl.pallas_call(functools.partial(kernel, nx, ny), out_shape=(jax.ShapeDty...  63.5 us
    sub x1, other arithmetic, body(): return (mu + step, lam - corr)  2.15 us
    add x1, other arithmetic, body(): return (mu + step, lam - corr)  1.84 us

profile of v6, /device:TPU:99, one launch (start us, length us, event | category | flops | bytes accessed | tf_op | source)
XLA Modules:
  0.0 68.8 jit_solution(9929243188420080667)
XLA Ops:
  1.3 63.5 %shard_map.68 = (f32[16,8,512]{2,1,0:T(8,128)}, f32[16,8,512]{2,1,0:T(8,128)}, f32[3,16,8,512]{3,2,1,0:T(8,128)}, f32[3,16,8,512]{3,2,1,0:T(8,128)}) custom-call(s32[1,1]{1,0:T(1,128)S(6)} %copy.7.bw_ref, f32[16,8,512]{2,1,0:T(8,128)} %dmg_ref.1, f32[3,16,8,512]{3,2,1,0:T(8,128)} %strain_ref.1, f32[16,8,512]{2,1,0:T(8,128)} %sd_ref.1, ...), custom_call_target="tpu_custom_call" | custom-call | tf_op jit(solution)/shard_map/pallas_call | solution.py:269
  64.8 0.0 copy-start
  64.8 1.8 %add.3 = f32[16,8,512]{2,1,0:T(8,128)} add(f32[16,8,512]{2,1,0:T(8,128)} %get-tuple-element.6, f32[16,8,512]{2,1,0:T(8,128)} %get-tuple-element.7) | non-fusion elementwise | flops 65536 | bytes 786432 | tf_op jit(solution)/shard_map/add | solution.py:297
  66.6 0.0 copy-done
  66.6 2.2 %sub.3 = f32[3,16,8,512]{3,2,1,0:T(8,128)} subtract(f32[3,16,8,512]{3,2,1,0:T(8,128)S(1)} %copy-done, f32[3,16,8,512]{3,2,1,0:T(8,128)} %get-tuple-element.9) | non-fusion elementwise | flops 196608 | bytes 2359296 | tf_op jit(solution)/shard_map/sub | solution.py:297
Async XLA Ops:
  64.8 1.9 %copy-start = (f32[3,16,8,512]{3,2,1,0:T(8,128)S(1)}, f32[3,16,8,512]{3,2,1,0:T(8,128)}, u32[]{:S(2)}) copy-start(f32[3,16,8,512]{3,2,1,0:T(8,128)} %get-tuple-element.8) | copy-start | bytes 2359300

commit v7 on v6

--- a/solution.py
+++ b/solution.py
@@ -293,8 +293,21 @@
             collective_id=0, has_side_effects=True, vmem_limit_bytes=60 * 1024 * 1024
         ),
     )(brick_work, damage, strain, seed_damage, seed_disp)
-    mu, step, lam, corr = state
-    return mu + step, lam - corr
+    return pl.pallas_call(
+        finish_kernel,
+        out_shape=(
+            jax.ShapeDtypeStruct((X, Y, Z), f32),
+            jax.ShapeDtypeStruct((3, X, Y, Z), f32),
+        ),
+        in_specs=[vmem] * 4,
+        out_specs=(vmem, vmem),
+    )(*state)
+
+
+def finish_kernel(mu_ref, step_ref, lam_ref, corr_ref, out_mu_ref, out_disp_ref):
+    out_mu_ref[...] = mu_ref[...] + step_ref[...]
+    for c in range(3):
+        out_disp_ref[c] = lam_ref[c] - corr_ref[c]
 
 
 def solution(mesh):

time: 69 us -> 67.5 us (0.978)
  other arithmetic: 3.99 us -> 0 us
  Pallas kernels: 63.5 us -> 66 us
    pallas_call x0 -> x1, Pallas kernels: none -> 2.53 us  [body(): pl.pallas_call(finish_kernel, out_shape=(jax.ShapeDtypeStruct((X, Y, Z),...]
    sub x1 -> x0, other arithmetic: 2.15 us -> none  [body(): return (mu + step, lam - corr)]
    add x1 -> x0, other arithmetic: 1.84 us -> none  [body(): return (mu + step, lam - corr)]
where the time goes in v7:
time: 67.5 us; the launch traced here: 67.3 us
  Pallas kernels  66 us (98%)
  between operations  1.29 us (2%)
    pallas_call x1, Pallas kernels, body(): pl.pallas_call(functools.partial(kernel, nx, ny), out_shape=(jax.ShapeDty...  63.5 us
    pallas_call x1, Pallas kernels, body(): pl.pallas_call(finish_kernel, out_shape=(jax.ShapeDtypeStruct((X, Y, Z),...  2.53 us

profile of v7, /device:TPU:99, one launch (start us, length us, event | category | flops | bytes accessed | tf_op | source)
XLA Modules:
  0.0 67.3 jit_solution(16317134171476070998)
XLA Ops:
  1.3 63.5 %shard_map.68 = (f32[16,8,512]{2,1,0:T(8,128)}, f32[16,8,512]{2,1,0:T(8,128)}, f32[3,16,8,512]{3,2,1,0:T(8,128)}, f32[3,16,8,512]{3,2,1,0:T(8,128)}) custom-call(s32[1,1]{1,0:T(1,128)S(6)} %copy.7.bw_ref, f32[16,8,512]{2,1,0:T(8,128)} %dmg_ref.1, f32[3,16,8,512]{3,2,1,0:T(8,128)} %strain_ref.1, f32[16,8,512]{2,1,0:T(8,128)} %sd_ref.1, ...), custom_call_target="tpu_custom_call" | custom-call | tf_op jit(solution)/shard_map/pallas_call | solution.py:269
  64.8 2.5 %shard_map.69 = (f32[16,8,512]{2,1,0:T(8,128)}, f32[3,16,8,512]{3,2,1,0:T(8,128)}) custom-call(f32[16,8,512]{2,1,0:T(8,128)} %get-tuple-element.6.mu_ref, f32[16,8,512]{2,1,0:T(8,128)} %get-tuple-element.7.step_ref, f32[3,16,8,512]{3,2,1,0:T(8,128)} %get-tuple-element.8.lam_ref, f32[3,16,8,512]{3,2,1,0:T(8,128)} %get-tuple-element.9.corr_ref), custom_call_target="tpu_custom_call" | custom-call | tf_op jit(solution)/shard_map/pallas_call | solution.py:296

commit v8 on v3

--- a/solution.py
+++ b/solution.py
@@ -264,7 +264,7 @@
     X, Y, Z = damage.shape
     f32 = jnp.float32
     vmem = pl.BlockSpec(memory_space=pltpu.VMEM)
-    return pl.pallas_call(
+    state = pl.pallas_call(
         functools.partial(kernel, nx, ny),
         out_shape=(
             jax.ShapeDtypeStruct((X, Y, Z), f32),
@@ -289,6 +289,21 @@
             collective_id=0, has_side_effects=True, vmem_limit_bytes=60 * 1024 * 1024
         ),
     )(brick_work, damage, strain, seed_damage, seed_disp)
+    return pl.pallas_call(
+        pass_kernel,
+        out_shape=(
+            jax.ShapeDtypeStruct((X, Y, Z), f32),
+            jax.ShapeDtypeStruct((3, X, Y, Z), f32),
+        ),
+        in_specs=[vmem, vmem],
+        out_specs=(vmem, vmem),
+    )(*state)
+
+
+def pass_kernel(mu_ref, disp_ref, out_mu_ref, out_disp_ref):
+    out_mu_ref[...] = mu_ref[...]
+    for c in range(3):
+        out_disp_ref[c] = disp_ref[c]
 
 
 def solution(mesh):

time: 68.5 us -> 66.9 us (0.977)
  the two profiles are of different devices: /device:TPU:26 before, /device:TPU:99 now
where the time goes in v8:
time: 66.9 us; the launch traced here: 66.7 us
  Pallas kernels  65.4 us (98%)
  between operations  1.29 us (2%)
    pallas_call x1, Pallas kernels, body(): pl.pallas_call(functools.partial(kernel, nx, ny), out_shape=(jax.ShapeDty...  63.2 us
    pallas_call x1, Pallas kernels, body(): pl.pallas_call(pass_kernel, out_shape=(jax.ShapeDtypeStruct((X, Y, Z), f3...  2.2 us

profile of v8, /device:TPU:99, one launch (start us, length us, event | category | flops | bytes accessed | tf_op | source)
XLA Modules:
  0.0 66.7 jit_solution(15053497372006004477)
XLA Ops:
  1.3 63.2 %shard_map.68 = (f32[16,8,512]{2,1,0:T(8,128)}, f32[3,16,8,512]{3,2,1,0:T(8,128)}) custom-call(s32[1,1]{1,0:T(1,128)S(6)} %copy.7.bw_ref, f32[16,8,512]{2,1,0:T(8,128)} %dmg_ref.1, f32[3,16,8,512]{3,2,1,0:T(8,128)} %strain_ref.1, f32[16,8,512]{2,1,0:T(8,128)} %sd_ref.1, f32[3,16,8,512]{3,2,1,0:T(8,128)} %sdisp_ref.1), custom_call_target="tpu_custom_call" | custom-call | tf_op jit(solution)/shard_map/pallas_call | solution.py:267
  64.5 2.2 %shard_map.69 = (f32[16,8,512]{2,1,0:T(8,128)}, f32[3,16,8,512]{3,2,1,0:T(8,128)}) custom-call(f32[16,8,512]{2,1,0:T(8,128)} %get-tuple-element.4.mu_ref, f32[3,16,8,512]{3,2,1,0:T(8,128)} %get-tuple-element.5.disp_ref), custom_call_target="tpu_custom_call" | custom-call | tf_op jit(solution)/shard_map/pallas_call | solution.py:292

commit v9 on v8

--- a/solution.py
+++ b/solution.py
@@ -289,21 +289,23 @@
             collective_id=0, has_side_effects=True, vmem_limit_bytes=60 * 1024 * 1024
         ),
     )(brick_work, damage, strain, seed_damage, seed_disp)
+    mu_block = pl.BlockSpec((X // 4, Y, Z), lambda i: (i, 0, 0))
+    disp_block = pl.BlockSpec((3, X // 4, Y, Z), lambda i: (0, i, 0, 0))
     return pl.pallas_call(
         pass_kernel,
         out_shape=(
             jax.ShapeDtypeStruct((X, Y, Z), f32),
             jax.ShapeDtypeStruct((3, X, Y, Z), f32),
         ),
-        in_specs=[vmem, vmem],
-        out_specs=(vmem, vmem),
+        grid=(4,),
+        in_specs=[mu_block, disp_block],
+        out_specs=(mu_block, disp_block),
     )(*state)
 
 
 def pass_kernel(mu_ref, disp_ref, out_mu_ref, out_disp_ref):
     out_mu_ref[...] = mu_ref[...]
-    for c in range(3):
-        out_disp_ref[c] = disp_ref[c]
+    out_disp_ref[...] = disp_ref[...]
 
 
 def solution(mesh):

time: 66.9 us -> 68.1 us (1.018)
  Pallas kernels: 65.4 us -> 66.6 us
    pallas_call x1, Pallas kernels: 2.2 us -> 3.4 us  [body(): pl.pallas_call(pass_kernel, out_shape=(jax.ShapeDtypeStruct((X, Y, Z), f3...]
where the time goes in v9:
time: 68.1 us; the launch traced here: 67.9 us
  Pallas kernels  66.6 us (98%)
  between operations  1.29 us (2%)
    pallas_call x1, Pallas kernels, body(): pl.pallas_call(functools.partial(kernel, nx, ny), out_shape=(jax.ShapeDty...  63.2 us
    pallas_call x1, Pallas kernels, body(): pl.pallas_call(pass_kernel, out_shape=(jax.ShapeDtypeStruct((X, Y, Z), f3...  3.4 us

profile of v9, /device:TPU:99, one launch (start us, length us, event | category | flops | bytes accessed | tf_op | source)
XLA Modules:
  0.0 67.9 jit_solution(171620570014852632)
XLA Ops:
  1.3 63.2 %shard_map.68 = (f32[16,8,512]{2,1,0:T(8,128)}, f32[3,16,8,512]{3,2,1,0:T(8,128)}) custom-call(s32[1,1]{1,0:T(1,128)S(6)} %copy.7.bw_ref, f32[16,8,512]{2,1,0:T(8,128)} %dmg_ref.1, f32[3,16,8,512]{3,2,1,0:T(8,128)} %strain_ref.1, f32[16,8,512]{2,1,0:T(8,128)} %sd_ref.1, f32[3,16,8,512]{3,2,1,0:T(8,128)} %sdisp_ref.1), custom_call_target="tpu_custom_call" | custom-call | tf_op jit(solution)/shard_map/pallas_call | solution.py:267
  64.5 3.4 %shard_map.69 = (f32[16,8,512]{2,1,0:T(8,128)}, f32[3,16,8,512]{3,2,1,0:T(8,128)}) custom-call(f32[16,8,512]{2,1,0:T(8,128)} %get-tuple-element.4.mu_ref, f32[3,16,8,512]{3,2,1,0:T(8,128)} %get-tuple-element.5.disp_ref), custom_call_target="tpu_custom_call" | custom-call | tf_op jit(solution)/shard_map/pallas_call | solution.py:294

commit v10 on v8

--- a/solution.py
+++ b/solution.py
@@ -289,21 +289,26 @@
             collective_id=0, has_side_effects=True, vmem_limit_bytes=60 * 1024 * 1024
         ),
     )(brick_work, damage, strain, seed_damage, seed_disp)
+    hbm = pl.BlockSpec(memory_space=pl.ANY)
     return pl.pallas_call(
         pass_kernel,
         out_shape=(
             jax.ShapeDtypeStruct((X, Y, Z), f32),
             jax.ShapeDtypeStruct((3, X, Y, Z), f32),
         ),
-        in_specs=[vmem, vmem],
-        out_specs=(vmem, vmem),
+        in_specs=[hbm, hbm],
+        out_specs=(hbm, hbm),
+        scratch_shapes=[pltpu.SemaphoreType.DMA((2,))],
     )(*state)
 
 
-def pass_kernel(mu_ref, disp_ref, out_mu_ref, out_disp_ref):
-    out_mu_ref[...] = mu_ref[...]
-    for c in range(3):
-        out_disp_ref[c] = disp_ref[c]
+def pass_kernel(mu_ref, disp_ref, out_mu_ref, out_disp_ref, sems):
+    first = pltpu.make_async_copy(mu_ref, out_mu_ref, sems.at[0])
+    second = pltpu.make_async_copy(disp_ref, out_disp_ref, sems.at[1])
+    first.start()
+    second.start()
+    first.wait()
+    second.wait()
 
 
 def solution(mesh):

time: 66.9 us -> 97.5 us (1.46)
  Pallas kernels: 65.4 us -> 96.1 us
    pallas_call x1, Pallas kernels: 2.2 us -> 32.9 us  [body(): pl.pallas_call(pass_kernel, out_shape=(jax.ShapeDtypeStruct((X, Y, Z), f3...]
where the time goes in v10:
time: 97.5 us; the launch traced here: 97.4 us
  Pallas kernels  96.1 us (99%)
  between operations  1.29 us (1%)
    pallas_call x1, Pallas kernels, body(): pl.pallas_call(functools.partial(kernel, nx, ny), out_shape=(jax.ShapeDty...  63.2 us
    pallas_call x1, Pallas kernels, body(): pl.pallas_call(pass_kernel, out_shape=(jax.ShapeDtypeStruct((X, Y, Z), f3...  32.9 us

profile of v10, /device:TPU:99, one launch (start us, length us, event | category | flops | bytes accessed | tf_op | source)
XLA Modules:
  0.0 97.4 jit_solution(14619005539484136409)
XLA Ops:
  1.3 63.2 %shard_map.68 = (f32[16,8,512]{2,1,0:T(8,128)}, f32[3,16,8,512]{3,2,1,0:T(8,128)}) custom-call(s32[1,1]{1,0:T(1,128)S(6)} %copy.7.bw_ref, f32[16,8,512]{2,1,0:T(8,128)} %dmg_ref.1, f32[3,16,8,512]{3,2,1,0:T(8,128)} %strain_ref.1, f32[16,8,512]{2,1,0:T(8,128)} %sd_ref.1, f32[3,16,8,512]{3,2,1,0:T(8,128)} %sdisp_ref.1), custom_call_target="tpu_custom_call" | custom-call | tf_op jit(solution)/shard_map/pallas_call | solution.py:267
  64.5 32.9 %shard_map.69 = (f32[16,8,512]{2,1,0:T(8,128)}, f32[3,16,8,512]{3,2,1,0:T(8,128)}) custom-call(f32[16,8,512]{2,1,0:T(8,128)} %get-tuple-element.4.mu_ref, f32[3,16,8,512]{3,2,1,0:T(8,128)} %get-tuple-element.5.disp_ref), custom_call_target="tpu_custom_call" | custom-call | tf_op jit(solution)/shard_map/pallas_call | solution.py:293

commit v11 on v8

--- a/solution.py
+++ b/solution.py
@@ -30,9 +30,10 @@
 
 def kernel(
     nx, ny,
-    bw_ref, dmg_ref, strain_ref, sd_ref, sdisp_ref,
+    bw_ref, dmg_hbm, strain_hbm, sd_hbm, sdisp_hbm,
     out_mu_ref, out_disp_ref,
     dfr, dyl, dyh, sfr, syl, syh, faces, upd, invs, send_sem, recv_sem,
+    dmg_ref, strain_ref, sd_ref, sdisp_ref, load_sem,
 ):
     X, Y, Z = dmg_ref.shape
     bx = lax.axis_index("gx")
@@ -67,6 +68,15 @@
         def _():
             pl.semaphore_signal(barrier, inc=1, device_id=peers[d], device_id_type=MESH)
         count = count + has[d].astype(jnp.int32)
+    loads = [
+        pltpu.make_async_copy(src, dst, load_sem.at[k])
+        for k, (src, dst) in enumerate(((dmg_hbm, dmg_ref), (strain_hbm, strain_ref),
+                                        (sd_hbm, sd_ref), (sdisp_hbm, sdisp_ref)))
+    ]
+    for copy in loads:
+        copy.start()
+    for copy in loads:
+        copy.wait()
     pl.semaphore_wait(barrier, count)
 
     def exchange(slot, routes):
@@ -270,7 +280,7 @@
             jax.ShapeDtypeStruct((X, Y, Z), f32),
             jax.ShapeDtypeStruct((3, X, Y, Z), f32),
         ),
-        in_specs=[pl.BlockSpec(memory_space=pltpu.SMEM), vmem, vmem, vmem, vmem],
+        in_specs=[pl.BlockSpec(memory_space=pltpu.SMEM)] + [pl.BlockSpec(memory_space=pl.ANY)] * 4,
         out_specs=(vmem, vmem),
         scratch_shapes=[
             pltpu.VMEM((2, X + 2, Y, Z), f32),
@@ -284,6 +294,11 @@
             pltpu.VMEM((3, X, Y, Z), f32),
             pltpu.SemaphoreType.DMA((2 + SWEEPS, 4)),
             pltpu.SemaphoreType.DMA((2 + SWEEPS, 4)),
+            pltpu.VMEM((X, Y, Z), f32),
+            pltpu.VMEM((3, X, Y, Z), f32),
+            pltpu.VMEM((X, Y, Z), f32),
+            pltpu.VMEM((3, X, Y, Z), f32),
+            pltpu.SemaphoreType.DMA((4,)),
         ],
         compiler_params=pltpu.CompilerParams(
             collective_id=0, has_side_effects=True, vmem_limit_bytes=60 * 1024 * 1024

time: 66.9 us -> 66.2 us (0.990)
  the two profiles are of different devices: /device:TPU:99 before, /device:TPU:26 now
where the time goes in v11:
time: 66.2 us; the launch traced here: 66 us
  Pallas kernels  64.7 us (98%)
  between operations  1.29 us (2%)
    pallas_call x1, Pallas kernels, body(): pl.pallas_call(functools.partial(kernel, nx, ny), out_shape=(jax.ShapeDty...  62.5 us
    pallas_call x1, Pallas kernels, body(): pl.pallas_call(pass_kernel, out_shape=(jax.ShapeDtypeStruct((X, Y, Z), f3...  2.2 us

profile of v11, /device:TPU:26, one launch (start us, length us, event | category | flops | bytes accessed | tf_op | source)
XLA Modules:
  0.0 66.0 jit_solution(2404079789888291819)
XLA Ops:
  1.3 62.5 %shard_map.68 = (f32[16,8,512]{2,1,0:T(8,128)}, f32[3,16,8,512]{3,2,1,0:T(8,128)}) custom-call(s32[1,1]{1,0:T(1,128)S(6)} %copy.7.bw_ref, f32[16,8,512]{2,1,0:T(8,128)} %dmg_hbm.1, f32[3,16,8,512]{3,2,1,0:T(8,128)} %strain_hbm.1, f32[16,8,512]{2,1,0:T(8,128)} %sd_hbm.1, f32[3,16,8,512]{3,2,1,0:T(8,128)} %sdisp_hbm.1), custom_call_target="tpu_custom_call" | custom-call | tf_op jit(solution)/shard_map/pallas_call | solution.py:277
  63.8 2.2 %shard_map.69 = (f32[16,8,512]{2,1,0:T(8,128)}, f32[3,16,8,512]{3,2,1,0:T(8,128)}) custom-call(f32[16,8,512]{2,1,0:T(8,128)} %get-tuple-element.4.mu_ref, f32[3,16,8,512]{3,2,1,0:T(8,128)} %get-tuple-element.5.disp_ref), custom_call_target="tpu_custom_call" | custom-call | tf_op jit(solution)/shard_map/pallas_call | solution.py:307

commit v12 on v11

--- a/solution.py
+++ b/solution.py
@@ -31,9 +31,9 @@
 def kernel(
     nx, ny,
     bw_ref, dmg_hbm, strain_hbm, sd_hbm, sdisp_hbm,
-    out_mu_ref, out_disp_ref,
+    out_mu_hbm, out_disp_hbm,
     dfr, dyl, dyh, sfr, syl, syh, faces, upd, invs, send_sem, recv_sem,
-    dmg_ref, strain_ref, sd_ref, sdisp_ref, load_sem,
+    dmg_ref, strain_ref, sd_ref, sdisp_ref, load_sem, out_mu_ref, out_disp_ref, out_sem,
 ):
     X, Y, Z = dmg_ref.shape
     bx = lax.axis_index("gx")
@@ -262,9 +262,26 @@
             return carry
 
         lax.fori_loop(1, X - 1, step, 0)
+        if last:
+            outs = [
+                pltpu.make_async_copy(out_mu_ref.at[1:X - 1], out_mu_hbm.at[1:X - 1], out_sem.at[0]),
+                pltpu.make_async_copy(out_disp_ref.at[:, 1:X - 1], out_disp_hbm.at[:, 1:X - 1], out_sem.at[1]),
+            ]
+            for copy in outs:
+                copy.start()
         arrive(copies, (0, 1))
         for i in (0, X - 1):
             step(i, 0)
+        if last:
+            for k, i in enumerate((0, X - 1)):
+                outs.append(pltpu.make_async_copy(
+                    out_mu_ref.at[i:i + 1], out_mu_hbm.at[i:i + 1], out_sem.at[2 + 2 * k]))
+                outs.append(pltpu.make_async_copy(
+                    out_disp_ref.at[:, i:i + 1], out_disp_hbm.at[:, i:i + 1], out_sem.at[3 + 2 * k]))
+                outs[-2].start()
+                outs[-1].start()
+            for copy in outs:
+                copy.wait()
 
     for copies in pending:
         sent(copies)
@@ -281,7 +298,7 @@
             jax.ShapeDtypeStruct((3, X, Y, Z), f32),
         ),
         in_specs=[pl.BlockSpec(memory_space=pltpu.SMEM)] + [pl.BlockSpec(memory_space=pl.ANY)] * 4,
-        out_specs=(vmem, vmem),
+        out_specs=(pl.BlockSpec(memory_space=pl.ANY),) * 2,
         scratch_shapes=[
             pltpu.VMEM((2, X + 2, Y, Z), f32),
             pltpu.VMEM((2, X, 1, Z), f32),
@@ -299,6 +316,9 @@
             pltpu.VMEM((X, Y, Z), f32),
             pltpu.VMEM((3, X, Y, Z), f32),
             pltpu.SemaphoreType.DMA((4,)),
+            pltpu.VMEM((X, Y, Z), f32),
+            pltpu.VMEM((3, X, Y, Z), f32),
+            pltpu.SemaphoreType.DMA((6,)),
         ],
         compiler_params=pltpu.CompilerParams(
             collective_id=0, has_side_effects=True, vmem_limit_bytes=60 * 1024 * 1024

time: 66.2 us -> 66 us (level)
  no operation moved by 1% of the time
where the time goes in v12:
time: 66 us; the launch traced here: 65.8 us
  Pallas kernels  64.5 us (98%)
  between operations  1.29 us (2%)
    pallas_call x1, Pallas kernels, body(): pl.pallas_call(functools.partial(kernel, nx, ny), out_shape=(jax.ShapeDty...  62.3 us
    pallas_call x1, Pallas kernels, body(): pl.pallas_call(pass_kernel, out_shape=(jax.ShapeDtypeStruct((X, Y, Z), f3...  2.2 us

profile of v12, /device:TPU:26, one launch (start us, length us, event | category | flops | bytes accessed | tf_op | source)
XLA Modules:
  0.0 65.8 jit_solution(16041492936830956903)
XLA Ops:
  1.3 62.3 %shard_map.68 = (f32[16,8,512]{2,1,0:T(8,128)}, f32[3,16,8,512]{3,2,1,0:T(8,128)}) custom-call(s32[1,1]{1,0:T(1,128)S(6)} %copy.7.bw_ref, f32[16,8,512]{2,1,0:T(8,128)} %dmg_hbm.1, f32[3,16,8,512]{3,2,1,0:T(8,128)} %strain_hbm.1, f32[16,8,512]{2,1,0:T(8,128)} %sd_hbm.1, f32[3,16,8,512]{3,2,1,0:T(8,128)} %sdisp_hbm.1), custom_call_target="tpu_custom_call" | custom-call | tf_op jit(solution)/shard_map/pallas_call | solution.py:294
  63.6 2.2 %shard_map.69 = (f32[16,8,512]{2,1,0:T(8,128)}, f32[3,16,8,512]{3,2,1,0:T(8,128)}) custom-call(f32[16,8,512]{2,1,0:T(8,128)} %get-tuple-element.4.mu_ref, f32[3,16,8,512]{3,2,1,0:T(8,128)} %get-tuple-element.5.disp_ref), custom_call_target="tpu_custom_call" | custom-call | tf_op jit(solution)/shard_map/pallas_call | solution.py:327

commit v13 on v11

--- a/solution.py
+++ b/solution.py
@@ -310,15 +310,21 @@
             jax.ShapeDtypeStruct((X, Y, Z), f32),
             jax.ShapeDtypeStruct((3, X, Y, Z), f32),
         ),
-        in_specs=[vmem, vmem],
+        in_specs=[pl.BlockSpec(memory_space=pl.ANY)] * 2,
         out_specs=(vmem, vmem),
+        scratch_shapes=[pltpu.SemaphoreType.DMA((2,))],
     )(*state)
 
 
-def pass_kernel(mu_ref, disp_ref, out_mu_ref, out_disp_ref):
-    out_mu_ref[...] = mu_ref[...]
-    for c in range(3):
-        out_disp_ref[c] = disp_ref[c]
+def pass_kernel(mu_ref, disp_ref, out_mu_ref, out_disp_ref, sems):
+    copies = [
+        pltpu.make_async_copy(mu_ref, out_mu_ref, sems.at[0]),
+        pltpu.make_async_copy(disp_ref, out_disp_ref, sems.at[1]),
+    ]
+    for copy in copies:
+        copy.start()
+    for copy in copies:
+        copy.wait()
 
 
 def solution(mesh):

time: 66.2 us -> 66.2 us (level)
  no operation moved by 1% of the time
where the time goes in v13:
time: 66.2 us; the launch traced here: 66 us
  Pallas kernels  64.7 us (98%)
  between operations  1.29 us (2%)
    pallas_call x1, Pallas kernels, body(): pl.pallas_call(functools.partial(kernel, nx, ny), out_shape=(jax.ShapeDty...  62.5 us
    pallas_call x1, Pallas kernels, body(): pl.pallas_call(pass_kernel, out_shape=(jax.ShapeDtypeStruct((X, Y, Z), f3...  2.2 us

profile of v13, /device:TPU:26, one launch (start us, length us, event | category | flops | bytes accessed | tf_op | source)
XLA Modules:
  0.0 66.0 jit_solution(2097835526343439906)
XLA Ops:
  1.3 62.5 %shard_map.68 = (f32[16,8,512]{2,1,0:T(8,128)}, f32[3,16,8,512]{3,2,1,0:T(8,128)}) custom-call(s32[1,1]{1,0:T(1,128)S(6)} %copy.7.bw_ref, f32[16,8,512]{2,1,0:T(8,128)} %dmg_hbm.1, f32[3,16,8,512]{3,2,1,0:T(8,128)} %strain_hbm.1, f32[16,8,512]{2,1,0:T(8,128)} %sd_hbm.1, f32[3,16,8,512]{3,2,1,0:T(8,128)} %sdisp_hbm.1), custom_call_target="tpu_custom_call" | custom-call | tf_op jit(solution)/shard_map/pallas_call | solution.py:277
  63.8 2.2 %shard_map.69 = (f32[16,8,512]{2,1,0:T(8,128)}, f32[3,16,8,512]{3,2,1,0:T(8,128)}) custom-call(f32[16,8,512]{2,1,0:T(8,128)} %get-tuple-element.4.mu_ref, f32[3,16,8,512]{3,2,1,0:T(8,128)} %get-tuple-element.5.disp_ref), custom_call_target="tpu_custom_call" | custom-call | tf_op jit(solution)/shard_map/pallas_call | solution.py:307

commit v14 on v13

--- a/solution.py
+++ b/solution.py
@@ -77,6 +77,23 @@
         copy.start()
     for copy in loads:
         copy.wait()
+    dfr[0, 1:X + 1] = dmg_ref[...]
+    dfr[1, 1:X + 1] = strain_ref[0]
+
+    def local(i, carry):
+        sx = strain_ref[0, i]
+        sy = strain_ref[1, i]
+        sz = strain_ref[2, i]
+        energy = 0.5 * (sx * sx + sy * sy + sz * sz)
+        inv_mu = 1.0 / (TOUGH_OVER_LENGTH + 2.0 * energy + 6.0 * TOUGH_TIMES_LENGTH)
+        invs[0, i] = inv_mu
+        invs[2, i] = TOUGH_OVER_LENGTH + 2.0 * energy
+        mu0 = inv_mu * sd_ref[i] / CENTER_VALUE
+        upd[0, i] = mu0
+        sfr[0, 0, i + 1] = mu0
+        return carry
+
+    lax.fori_loop(0, X, local, 0)
     pl.semaphore_wait(barrier, count)
 
     def exchange(slot, routes):
@@ -121,8 +138,6 @@
         (strain_ref.at[1, :, Y - 1:Y], dyl.at[1]),
         (strain_ref.at[1, :, 0:1], dyh.at[1]),
     ))
-    dfr[0, 1:X + 1] = dmg_ref[...]
-    dfr[1, 1:X + 1] = strain_ref[0]
     arrive(c_dmg, (2, 3))
     arrive(c_str, (2, 3))
     pending = [c_dmg, c_str]
@@ -150,18 +165,8 @@
             faces[k, i] = fs[k]
             if k:
                 total = total + fs[k]
-        sx = strain_ref[0, i]
-        sy = strain_ref[1, i]
-        sz = strain_ref[2, i]
-        energy = 0.5 * (sx * sx + sy * sy + sz * sz)
-        inv_mu = 1.0 / (TOUGH_OVER_LENGTH + 2.0 * energy + 6.0 * TOUGH_TIMES_LENGTH)
         inv_lam = 1.0 / (MASS_SHIFT + STIFF_SCALE * total)
-        invs[0, i] = inv_mu
         invs[1, i] = inv_lam
-        invs[2, i] = TOUGH_OVER_LENGTH + 2.0 * energy
-        mu0 = inv_mu * sd_ref[i] / CENTER_VALUE
-        upd[0, i] = mu0
-        sfr[0, 0, i + 1] = mu0
         for c in range(3):
             lam0 = inv_lam * sdisp_ref[c, i] / CENTER_VALUE
             upd[1 + c, i] = lam0

time: 66.2 us -> 66.5 us (level)
  no operation moved by 1% of the time
where the time goes in v14:
time: 66.5 us; the launch traced here: 66.3 us
  Pallas kernels  65 us (98%)
  between operations  1.29 us (2%)
    pallas_call x1, Pallas kernels, body(): pl.pallas_call(functools.partial(kernel, nx, ny), out_shape=(jax.ShapeDty...  62.8 us
    pallas_call x1, Pallas kernels, body(): pl.pallas_call(pass_kernel, out_shape=(jax.ShapeDtypeStruct((X, Y, Z), f3...  2.2 us

profile of v14, /device:TPU:26, one launch (start us, length us, event | category | flops | bytes accessed | tf_op | source)
XLA Modules:
  0.0 66.3 jit_solution(13653953254913797512)
XLA Ops:
  1.3 62.8 %shard_map.68 = (f32[16,8,512]{2,1,0:T(8,128)}, f32[3,16,8,512]{3,2,1,0:T(8,128)}) custom-call(s32[1,1]{1,0:T(1,128)S(6)} %copy.7.bw_ref, f32[16,8,512]{2,1,0:T(8,128)} %dmg_hbm.1, f32[3,16,8,512]{3,2,1,0:T(8,128)} %strain_hbm.1, f32[16,8,512]{2,1,0:T(8,128)} %sd_hbm.1, f32[3,16,8,512]{3,2,1,0:T(8,128)} %sdisp_hbm.1), custom_call_target="tpu_custom_call" | custom-call | tf_op jit(solution)/shard_map/pallas_call | solution.py:282
  64.1 2.2 %shard_map.69 = (f32[16,8,512]{2,1,0:T(8,128)}, f32[3,16,8,512]{3,2,1,0:T(8,128)}) custom-call(f32[16,8,512]{2,1,0:T(8,128)} %get-tuple-element.4.mu_ref, f32[3,16,8,512]{3,2,1,0:T(8,128)} %get-tuple-element.5.disp_ref), custom_call_target="tpu_custom_call" | custom-call | tf_op jit(solution)/shard_map/pallas_call | solution.py:312

commit v15 on v13

--- a/solution.py
+++ b/solution.py
@@ -79,7 +79,7 @@
         copy.wait()
     pl.semaphore_wait(barrier, count)
 
-    def exchange(slot, routes):
+    def exchange(slot, routes, dirs=range(4)):
         copies = []
         for d in range(4):
             src, dst = routes[d]
@@ -90,11 +90,14 @@
                     device_id=peers[d], device_id_type=MESH,
                 )
             )
-        for d in range(4):
+        start(copies, dirs)
+        return copies
+
+    def start(copies, dirs):
+        for d in dirs:
             @pl.when(has[d])
             def _():
                 copies[d].start()
-        return copies
 
     def arrive(copies, dirs):
         opposite = (1, 0, 3, 2)
@@ -114,13 +117,16 @@
         (dmg_ref.at[0:1], dfr.at[0, X + 1:X + 2]),
         (dmg_ref.at[:, Y - 1:Y], dyl.at[0]),
         (dmg_ref.at[:, 0:1], dyh.at[0]),
-    ))
+    ), ())
     c_str = exchange(1, (
         (strain_ref.at[0, X - 1:X], dfr.at[1, 0:1]),
         (strain_ref.at[0, 0:1], dfr.at[1, X + 1:X + 2]),
         (strain_ref.at[1, :, Y - 1:Y], dyl.at[1]),
         (strain_ref.at[1, :, 0:1], dyh.at[1]),
-    ))
+    ), ())
+    for dirs in ((0, 1), (2, 3)):
+        start(c_dmg, dirs)
+        start(c_str, dirs)
     dfr[0, 1:X + 1] = dmg_ref[...]
     dfr[1, 1:X + 1] = strain_ref[0]
     arrive(c_dmg, (2, 3))

time: 66.2 us -> 65.7 us (level)
  no operation moved by 1% of the time
where the time goes in v15:
time: 65.7 us; the launch traced here: 65.5 us
  Pallas kernels  64.2 us (98%)
  between operations  1.29 us (2%)
    pallas_call x1, Pallas kernels, body(): pl.pallas_call(functools.partial(kernel, nx, ny), out_shape=(jax.ShapeDty...  62 us
    pallas_call x1, Pallas kernels, body(): pl.pallas_call(pass_kernel, out_shape=(jax.ShapeDtypeStruct((X, Y, Z), f3...  2.2 us

profile of v15, /device:TPU:26, one launch (start us, length us, event | category | flops | bytes accessed | tf_op | source)
XLA Modules:
  0.0 65.5 jit_solution(3358407601013590268)
XLA Ops:
  1.3 62.0 %shard_map.68 = (f32[16,8,512]{2,1,0:T(8,128)}, f32[3,16,8,512]{3,2,1,0:T(8,128)}) custom-call(s32[1,1]{1,0:T(1,128)S(6)} %copy.7.bw_ref, f32[16,8,512]{2,1,0:T(8,128)} %dmg_hbm.1, f32[3,16,8,512]{3,2,1,0:T(8,128)} %strain_hbm.1, f32[16,8,512]{2,1,0:T(8,128)} %sd_hbm.1, f32[3,16,8,512]{3,2,1,0:T(8,128)} %sdisp_hbm.1), custom_call_target="tpu_custom_call" | custom-call | tf_op jit(solution)/shard_map/pallas_call | solution.py:283
  63.3 2.2 %shard_map.69 = (f32[16,8,512]{2,1,0:T(8,128)}, f32[3,16,8,512]{3,2,1,0:T(8,128)}) custom-call(f32[16,8,512]{2,1,0:T(8,128)} %get-tuple-element.4.mu_ref, f32[3,16,8,512]{3,2,1,0:T(8,128)} %get-tuple-element.5.disp_ref), custom_call_target="tpu_custom_call" | custom-call | tf_op jit(solution)/shard_map/pallas_call | solution.py:313

commit v16 on v13

--- a/solution.py
+++ b/solution.py
@@ -312,14 +312,13 @@
         ),
         in_specs=[pl.BlockSpec(memory_space=pl.ANY)] * 2,
         out_specs=(vmem, vmem),
-        scratch_shapes=[pltpu.SemaphoreType.DMA((2,))],
+        scratch_shapes=[pltpu.SemaphoreType.DMA((4,))],
     )(*state)
 
 
 def pass_kernel(mu_ref, disp_ref, out_mu_ref, out_disp_ref, sems):
-    copies = [
-        pltpu.make_async_copy(mu_ref, out_mu_ref, sems.at[0]),
-        pltpu.make_async_copy(disp_ref, out_disp_ref, sems.at[1]),
+    copies = [pltpu.make_async_copy(mu_ref, out_mu_ref, sems.at[0])] + [
+        pltpu.make_async_copy(disp_ref.at[c], out_disp_ref.at[c], sems.at[1 + c]) for c in range(3)
     ]
     for copy in copies:
         copy.start()

time: 66.2 us -> 66.2 us (level)
  no operation moved by 1% of the time
where the time goes in v16:
time: 66.2 us; the launch traced here: 66 us
  Pallas kernels  64.7 us (98%)
  between operations  1.29 us (2%)
    pallas_call x1, Pallas kernels, body(): pl.pallas_call(functools.partial(kernel, nx, ny), out_shape=(jax.ShapeDty...  62.5 us
    pallas_call x1, Pallas kernels, body(): pl.pallas_call(pass_kernel, out_shape=(jax.ShapeDtypeStruct((X, Y, Z), f3...  2.19 us

profile of v16, /device:TPU:26, one launch (start us, length us, event | category | flops | bytes accessed | tf_op | source)
XLA Modules:
  0.0 66.0 jit_solution(14188581465862605770)
XLA Ops:
  1.3 62.5 %shard_map.68 = (f32[16,8,512]{2,1,0:T(8,128)}, f32[3,16,8,512]{3,2,1,0:T(8,128)}) custom-call(s32[1,1]{1,0:T(1,128)S(6)} %copy.7.bw_ref, f32[16,8,512]{2,1,0:T(8,128)} %dmg_hbm.1, f32[3,16,8,512]{3,2,1,0:T(8,128)} %strain_hbm.1, f32[16,8,512]{2,1,0:T(8,128)} %sd_hbm.1, f32[3,16,8,512]{3,2,1,0:T(8,128)} %sdisp_hbm.1), custom_call_target="tpu_custom_call" | custom-call | tf_op jit(solution)/shard_map/pallas_call | solution.py:277
  63.8 2.2 %shard_map.69 = (f32[16,8,512]{2,1,0:T(8,128)}, f32[3,16,8,512]{3,2,1,0:T(8,128)}) custom-call(f32[16,8,512]{2,1,0:T(8,128)} %get-tuple-element.4.mu_ref, f32[3,16,8,512]{3,2,1,0:T(8,128)} %get-tuple-element.5.disp_ref), custom_call_target="tpu_custom_call" | custom-call | tf_op jit(solution)/shard_map/pallas_call | solution.py:307
